TPU v7x, 256 devices: a whole 4x4x8 slice. The times are simulated.
256 devices in a mesh: row: 32 (over y, x, z_hi), col: 8 (over z_lo, core).
Axes of the slice: x: 4, y: 4, z: 8 (z_hi: 2, z_lo: 4; z = z_hi * 4 + z_lo), core: 2. Of those that a mesh axis runs over, the one named last changes fastest.
Arguments:
- alignment: bfloat16 [64, 1536, 256], P('row', 'col'), may hold values from -6 to 6
- pair_act: bfloat16 [1536, 1536, 128], P('row', 'col'), may hold values from -600 to 600
- targets: int32 [1536, 1536], P('row', 'col'), may hold values from 0 to 63, as said below
- crop_mask: int32 [1536], replicated, may hold values 0 or 1
- projection_weight: bfloat16 [256, 64], replicated, may hold values from -0.375 to 0.375
- w_outer: bfloat16 [1024, 128], replicated, may hold values from -1.5 to 1.5
- w_expand: bfloat16 [128, 512], replicated, may hold values from -0.5 to 0.5
- w_shrink: bfloat16 [512, 128], replicated, may hold values from -0.25 to 0.25
- w_bins: bfloat16 [128, 64], replicated, may hold values from -1.8 to 1.8
Outputs:
- pair_grad: bfloat16 [1536, 1536, 128], P('row', 'col')
Inputs may be any that keep to these rules, and one draw needn't show every extreme that they name: targets[i, j] equals targets[j, i].
All inputs are finite; a program needn't handle non-finite values.
Results may differ from a plain program's by a relative error of at most 0.02.
The roundings to bfloat16 on the way count: a program that leaves them out, or rounds other values in their place, can miss the bound.
Values may be sent and summed in bfloat16 or wider, within the bound.
A program may use at most 128 MiB of HBM per device.

v0:
```python
import jax
import jax.numpy as jnp
from jax import lax
from jax.sharding import PartitionSpec as P

FACTOR_CHANNELS = 32
BINS = 64
SEQUENCE_COUNT = 64


epsilon = 1e-05


def from_root(shard, axis, root):
    mine = lax.axis_index(axis) == root
    return lax.psum(jnp.where(mine, shard, jnp.zeros_like(shard)), axis)


def layer_normalize(values):
    average = jnp.mean(values, axis=-1, keepdims=True)
    centred = values - average
    inverse_deviation = lax.rsqrt(jnp.mean(centred * centred, axis=-1, keepdims=True) + epsilon)
    return (centred * inverse_deviation, inverse_deviation)


def norm_project(shard_rows, projection_weight):
    normed = layer_normalize(shard_rows.astype(jnp.float32))[0].astype(jnp.bfloat16)
    factor = jnp.dot(normed, projection_weight, preferred_element_type=jnp.float32).astype(
        jnp.bfloat16
    )
    return factor.reshape(shard_rows.shape[0], -1)


def mirrored(tile_rows, rows_dev, n_row, n_col):
    ratio = n_row // n_col
    group_rows = tile_rows.shape[0] // n_col
    sectioned = tile_rows.reshape(n_col, group_rows, ratio, rows_dev * BINS).transpose(0, 2, 1, 3)
    first_hop = lax.all_to_all(sectioned, "col", split_axis=0, concat_axis=0, tiled=True)
    regrouped = first_hop.reshape(n_row, 1, group_rows, rows_dev * BINS)
    arrived = lax.all_to_all(
        lax.all_to_all(regrouped, "row", split_axis=0, concat_axis=1, tiled=True),
        "col",
        split_axis=1,
        concat_axis=0,
        tiled=True,
    )
    return arrived.reshape(n_col, ratio, group_rows, rows_dev, BINS).transpose(3, 1, 0, 2, 4)


def per_device(
    alignment, pair_act, targets, crop_mask, projection_weight, w_outer, w_expand, w_shrink, w_bins
):
    rows_dev, cols_dev, channels = pair_act.shape
    n_row = lax.axis_size("row")
    n_col = lax.axis_size("col")
    ratio = n_row // n_col
    row_index = lax.axis_index("row")
    col_index = lax.axis_index("col")
    factors = norm_project(lax.all_gather(alignment, "row", axis=0, tiled=True), projection_weight)
    factors = factors.reshape(SEQUENCE_COUNT, cols_dev, 2 * FACTOR_CHANNELS)
    right_side = factors[:, :, FACTOR_CHANNELS:]
    own_left = lax.dynamic_slice_in_dim(
        factors[:, :, :FACTOR_CHANNELS], row_index % ratio * rows_dev, rows_dev, 1
    )
    left_side = from_root(
        own_left.reshape(SEQUENCE_COUNT, rows_dev * FACTOR_CHANNELS), "col", row_index // ratio
    )
    left_side = left_side.reshape(SEQUENCE_COUNT, rows_dev, FACTOR_CHANNELS)
    block_rows = 8
    blocks = rows_dev // block_rows
    pair_blocks = pair_act.reshape(blocks, block_rows, cols_dev, channels)
    left_blocks = left_side.reshape(SEQUENCE_COUNT, blocks, block_rows, FACTOR_CHANNELS).transpose(
        1, 0, 2, 3
    )

    def forward_block(inputs):
        pair_rows, left_rows = inputs
        outer = (
            jnp.einsum("sic,sje->ijce", left_rows, right_side, preferred_element_type=jnp.float32)
            / SEQUENCE_COUNT
        )
        outer = outer.reshape(block_rows * cols_dev, FACTOR_CHANNELS * FACTOR_CHANNELS).astype(
            jnp.bfloat16
        )
        update = jnp.dot(outer, w_outer, preferred_element_type=jnp.float32)
        middle_state = (
            pair_rows.reshape(block_rows * cols_dev, channels).astype(jnp.float32) + update
        ).astype(jnp.bfloat16)
        xnorm = layer_normalize(middle_state.astype(jnp.float32))[0].astype(jnp.bfloat16)
        before = lax.optimization_barrier(
            jnp.dot(xnorm, w_expand, preferred_element_type=jnp.float32).astype(jnp.bfloat16)
        )
        hidden = jax.nn.silu(before.astype(jnp.float32)).astype(jnp.bfloat16)
        final = (
            middle_state.astype(jnp.float32)
            + jnp.dot(hidden, w_shrink, preferred_element_type=jnp.float32)
        ).astype(jnp.bfloat16)
        logits = jnp.dot(final, w_bins, preferred_element_type=jnp.float32).astype(jnp.bfloat16)
        return (middle_state, before, logits.reshape(block_rows, cols_dev * BINS))

    middle_state, before, logits = lax.map(forward_block, (pair_blocks, left_blocks))
    across = mirrored(logits.reshape(rows_dev, cols_dev * BINS), rows_dev, n_row, n_col).reshape(
        rows_dev, cols_dev, BINS
    )
    own = logits.reshape(rows_dev, cols_dev, BINS)
    scores = own.astype(jnp.float32) + across.astype(jnp.float32)
    scores = scores - jnp.max(scores, axis=-1, keepdims=True)
    expo = jnp.exp(scores)
    prob = expo / jnp.sum(expo, axis=-1, keepdims=True)
    onehot = (targets[:, :, None] == jnp.arange(BINS, dtype=jnp.int32)).astype(jnp.float32)
    row_mask = lax.dynamic_slice_in_dim(crop_mask, row_index * rows_dev, rows_dev).astype(
        jnp.float32
    )
    col_mask = lax.dynamic_slice_in_dim(crop_mask, col_index * cols_dev, cols_dev).astype(
        jnp.float32
    )
    weight = row_mask[:, None] * col_mask[None, :]
    dlogits = (2.0 * (prob - onehot) * weight[:, :, None]).astype(jnp.bfloat16)
    dlog_blocks = dlogits.reshape(blocks, block_rows * cols_dev, BINS)

    def backward_block(inputs):
        middle_row_block, before_rows, dlog_rows = inputs
        final_gradient = jnp.dot(dlog_rows, w_bins.T, preferred_element_type=jnp.float32)
        before_f = before_rows.astype(jnp.float32)
        sigma = jax.nn.sigmoid(before_f)
        slope = sigma * (1.0 + before_f * (1.0 - sigma))
        dhidden = (
            jnp.dot(
                final_gradient.astype(jnp.bfloat16), w_shrink.T, preferred_element_type=jnp.float32
            )
            * slope
        ).astype(jnp.bfloat16)
        normed_input_gradient = jnp.dot(dhidden, w_expand.T, preferred_element_type=jnp.float32)
        standardized_input, inverse_deviation = layer_normalize(
            middle_row_block.astype(jnp.float32)
        )
        middle_gradient = final_gradient + inverse_deviation * (
            normed_input_gradient
            - jnp.mean(normed_input_gradient, axis=-1, keepdims=True)
            - standardized_input
            * jnp.mean(normed_input_gradient * standardized_input, axis=-1, keepdims=True)
        )
        return middle_gradient.astype(jnp.bfloat16)

    grads = lax.map(backward_block, (middle_state, before, dlog_blocks))
    return grads.reshape(rows_dev, cols_dev, channels)


def solution(mesh):
    in_specs = (
        P("row", "col", None),
        P("row", "col", None),
        P("row", "col"),
        P(),
        P(),
        P(),
        P(),
        P(),
        P(),
    )
    out_specs = P("row", "col", None)
    return jax.shard_map(
        per_device, mesh=mesh, in_specs=in_specs, out_specs=out_specs, check_vma=False
    )
```

profile of v0, /device:TPU:1, one launch (start us, length us, event | category | flops | bytes accessed | tf_op | source)
XLA Modules:
  0.0 618.3 jit_solution(1737578397463702173)
XLA Ops:
  7.3 138.0 %all-gather.2.cloned.1.call-done = bf16[64,192,256]{2,1,0:T(8,128)(2,1)} async-done(((bf16[2,192,256]{2,1,0:T(8,128)(2,1)}), bf16[64,192,256]{2,1,0:T(8,128)(2,1)}) %all-gather.2.cloned.1.call-update) | async-done | bytes 6291472 | tf_op jit(solution)/shard_map/all_gather | solution.py:59
  145.3 5.2 convert_reduce_fusion.2
  150.5 4.4 fusion.54
  155.0 5.2 fusion.60
  164.0 62.7 %all-reduce.2.cloned.1.call-done = bf16[6,64,8,32]{1,3,2,0:T(8,128)(2,1)} async-done(((bf16[6,64,8,32]{1,3,2,0:T(8,128)(2,1)}), bf16[6,64,8,32]{1,3,2,0:T(8,128)(2,1)}) %all-reduce.2.cloned.1.call-update) | async-done | bytes 196624 | tf_op jit(solution)/shard_map/psum | solution.py:16
  226.7 158.3 %while.24 = (s32[]{:T(128)}, bf16[6,1536,128]{1,2,0:T(8,128)(2,1)}, bf16[6,1536,512]{2,1,0:T(8,128)(2,1)}, bf16[6,8,12288]{2,1,0:T(8,128)(2,1)}, bf16[6,8,192,12...) while((s32[]{:T(128)}, bf16[6,1536,128]{1,2,0:T(8,128)(2,1)}, ...), condition=%wide.region_6.7_spmd, body=%wide.region_3.6_spmd.sunk | while | flops 1043695104 | bytes 37036208 | solution.py:101
  229.2 4.5 copy.80
  233.7 6.3 %convert_element_type.284 = bf16[1536,1024]{0,1:T(8,128)(2,1)S(1)} reshape(bf16[8,192,32,32]{1,0,3,2:T(8,128)(2,1)} %copy.80) | data formatting | bytes 6291456 | tf_op jit(solution)/shard_map/while/body/eval_jaxpr/convert_element_type | solution.py:82
  255.6 4.5 copy.80
  260.1 6.3 %convert_element_type.284 = bf16[1536,1024]{0,1:T(8,128)(2,1)S(1)} reshape(bf16[8,192,32,32]{1,0,3,2:T(8,128)(2,1)} %copy.80) | data formatting | bytes 6291456 | tf_op jit(solution)/shard_map/while/body/eval_jaxpr/convert_element_type | solution.py:82
  282.0 4.5 copy.80
  286.5 6.3 %convert_element_type.284 = bf16[1536,1024]{0,1:T(8,128)(2,1)S(1)} reshape(bf16[8,192,32,32]{1,0,3,2:T(8,128)(2,1)} %copy.80) | data formatting | bytes 6291456 | tf_op jit(solution)/shard_map/while/body/eval_jaxpr/convert_element_type | solution.py:82
  308.3 4.5 copy.80
  312.8 6.3 %convert_element_type.284 = bf16[1536,1024]{0,1:T(8,128)(2,1)S(1)} reshape(bf16[8,192,32,32]{1,0,3,2:T(8,128)(2,1)} %copy.80) | data formatting | bytes 6291456 | tf_op jit(solution)/shard_map/while/body/eval_jaxpr/convert_element_type | solution.py:82
  334.7 4.5 copy.80
  339.2 6.3 %convert_element_type.284 = bf16[1536,1024]{0,1:T(8,128)(2,1)S(1)} reshape(bf16[8,192,32,32]{1,0,3,2:T(8,128)(2,1)} %copy.80) | data formatting | bytes 6291456 | tf_op jit(solution)/shard_map/while/body/eval_jaxpr/convert_element_type | solution.py:82
  361.1 4.5 copy.80
  365.6 6.3 %convert_element_type.284 = bf16[1536,1024]{0,1:T(8,128)(2,1)S(1)} reshape(bf16[8,192,32,32]{1,0,3,2:T(8,128)(2,1)} %copy.80) | data formatting | bytes 6291456 | tf_op jit(solution)/shard_map/while/body/eval_jaxpr/convert_element_type | solution.py:82
  387.0 34.3 %all_to_all.26 = bf16[8,4,6,3072]{3,1,2,0:T(4,128)(2,1)S(1)} all-to-all(bf16[8,4,6,3072]{3,1,2,0:T(4,128)(2,1)S(1)} %bitcast.140), channel_id=1, replica_groups=mesh['row'=32,'col'=8] {'col'}, dimensions={0} | all-to-all | bytes 2359296 | tf_op jit(solution)/shard_map/all_to_all | solution.py:38
  421.7 50.7 %all_to_all.27 = bf16[32,1,6,3072]{3,2,1,0:T(8,128)(2,1)} all-to-all(bf16[32,1,6,3072]{3,2,1,0:T(8,128)(2,1)S(1)} %bitcast.139), channel_id=1, replica_groups=mesh['row'=32,'col'=8] {'row'}, dimensions={0} | all-to-all | bytes 2359296 | tf_op jit(solution)/shard_map/all_to_all | solution.py:41
  472.4 7.7 %all-to-all-start.2 = ((bf16[1,32,6,3072]{3,2,0,1:T(8,128)(2,1)}), bf16[1,32,6,3072]{3,2,0,1:T(8,128)(2,1)}, u32[]{:S(2)}, u32[]{:S(2)}) async-start(bf16[1,32,6,3072]{3,2,0,1:T(8,128)(2,1)} %bitcast.20), calls=%async_computation.2 | async-start | bytes 3145728 | tf_op jit(solution)/shard_map/all_to_all | solution.py:40
  482.1 3.6 reshape.139
  485.8 3.5 reshape.137
  489.3 27.8 %all-to-all-done.2 = bf16[1,32,6,3072]{3,2,0,1:T(8,128)(2,1)} async-done(((bf16[1,32,6,3072]{3,2,0,1:T(8,128)(2,1)}), bf16[1,32,6,3072]{3,2,0,1:T(8,128)(2,1)}, u32[]{:S(2)}, u32[]{:S(2)}) %all-to-all-start.2) | async-done | bytes 1179680 | tf_op jit(solution)/shard_map/all_to_all | solution.py:40
  519.2 3.2 reshape.141
  522.4 3.0 copy.60
  528.6 4.7 exponential_reduce_fusion
  533.3 7.9 %copy.59 = f32[48,4,8,6,64]{4,3,2,1,0:T(8,128)} copy(f32[48,4,8,6,64]{4,0,1,2,3:T(8,128)} %bitcast.138) | data formatting | bytes 4718592 | tf_op jit(solution)/shard_map/convert_element_type | solution.py:106
  541.3 6.6 %reshape.138 = f32[6,1536,64]{2,1,0:T(8,128)} reshape(f32[48,4,8,6,64]{4,3,2,1,0:T(8,128)} %copy.59) | data formatting | bytes 4718592 | tf_op jit(solution)/shard_map/convert_element_type | solution.py:106
  547.9 8.4 %multiply_convert_fusion.1 = bf16[6,1536,64]{2,1,0:T(8,128)(2,1)} fusion(f32[6,1536,64]{2,1,0:T(8,128)} %reshape.137, f32[6,1536,64]{2,1,0:T(8,128)} %reshape.138, f32[6,1536]{1,0:T(8,128)S(1)} %multiply_multiply_fusion, s32[6,1536]{1,0:T(8,128)S(1)} %eq.22, f32[6,1536]{1,0:T(8,128)S(1)} %div.58, f32[6,1536]{1,0:T(8,128)S(1)} %sub.64), kind=kLoop, calls=%fused_computation.82 | loop fusion | flops 4718592 | bytes 6045696 | tf_op jit(solution)/shard_map/convert_element_type | solution.py:118
  556.3 54.4 %while.25 = (s32[]{:T(128)}, bf16[6,1536,128]{2,1,0:T(8,128)(2,1)}, bf16[6,1536,64]{2,1,0:T(8,128)(2,1)}, bf16[128,64]{0,1:T(8,128)(2,1)S(1)}, bf16[6,1536,128]{...) while((s32[]{:T(128)}, bf16[6,1536,128]{2,1,0:T(8,128)(2,1)}, ...), condition=%wide.region_14.15_spmd, body=%wide.region_9.14_spmd.sunk | while | flops 440010240 | bytes 12193377 | solution.py:145
  568.8 3.0 fusion.115
  (237 shorter events, 158.9 us)
Async XLA Ops:
  6.5 148.5 %copy-start = (bf16[256,64]{0,1:T(8,128)(2,1)S(1)}, bf16[256,64]{0,1:T(8,128)(2,1)}, u32[]{:S(2)}) copy-start(bf16[256,64]{0,1:T(8,128)(2,1)} %param.17) | copy-start | bytes 98308
  6.5 138.8 %all-gather.2.cloned.1.call-start = ((), (), s32[]{:S(2)}) async-start(), calls=%async_computation.3 | async-start | bytes 6488064 | tf_op jit(solution)/shard_map/all_gather | solution.py:59
  7.3 219.5 %all-reduce.2.cloned.1.call-start = ((), (), s32[]{:S(2)}) async-start(), calls=%async_computation.4 | async-start | bytes 786432 | tf_op jit(solution)/shard_map/psum | solution.py:16
  145.3 5.2 copy-start.3
  160.4 66.3 %copy-start.5 = (bf16[1024,128]{1,0:T(8,128)(2,1)S(1)}, bf16[1024,128]{1,0:T(8,128)(2,1)}, u32[]{:S(2)}) copy-start(bf16[1024,128]{1,0:T(8,128)(2,1)} %param.18) | copy-start | bytes 786436
  160.4 66.3 %copy-start.8 = (bf16[128,64]{0,1:T(8,128)(2,1)S(1)}, bf16[128,64]{0,1:T(8,128)(2,1)}, u32[]{:S(2)}) copy-start(bf16[128,64]{0,1:T(8,128)(2,1)} %param.21) | copy-start | bytes 49156
  244.3 3.3 copy-start.6
  246.9 0.7 copy-start.2
  270.7 3.3 copy-start.6
  273.3 0.7 copy-start.2
  297.1 3.3 copy-start.6
  299.6 0.7 copy-start.2
  323.4 3.3 copy-start.6
  326.0 0.7 copy-start.2
  349.8 3.3 copy-start.6
  352.4 0.7 copy-start.2
  376.1 3.3 copy-start.6
  378.7 0.7 copy-start.2
  421.7 60.3 %copy-start.9 = (s32[48,192]{1,0:T(8,128)S(1)}, s32[48,192]{1,0:T(8,128)}, u32[]{:S(2)}) copy-start(s32[48,192]{1,0:T(8,128)} %param.15) | copy-start | bytes 110596
  421.7 60.4 %copy-start.4 = (bf16[6,8,12288]{2,1,0:T(8,128)(2,1)S(1)}, bf16[6,8,12288]{2,1,0:T(8,128)(2,1)}, u32[]{:S(2)}) copy-start(bf16[6,8,12288]{2,1,0:T(8,128)(2,1)} %get-tuple-element.106) | copy-start | bytes 3538948
  472.4 44.7 %all-to-all-start.2 = ((bf16[1,32,6,3072]{3,2,0,1:T(8,128)(2,1)}), bf16[1,32,6,3072]{3,2,0,1:T(8,128)(2,1)}, u32[]{:S(2)}, u32[]{:S(2)}) async-start(bf16[1,32,6,3072]{3,2,0,1:T(8,128)(2,1)} %bitcast.20), calls=%async_computation.2 | async-start | bytes 3145728 | tf_op jit(solution)/shard_map/all_to_all | solution.py:40
  522.4 3.6 slice-start
  522.4 3.7 slice-start.1
  547.9 8.4 %copy-start.7 = (bf16[128,512]{1,0:T(8,128)(2,1)S(1)}, bf16[128,512]{1,0:T(8,128)(2,1)}, u32[]{:S(2)}) copy-start(bf16[128,512]{1,0:T(8,128)(2,1)} %get-tuple-element.426) | copy-start | bytes 393220
  547.9 8.4 %copy-start.10 = (bf16[512,128]{1,0:T(8,128)(2,1)S(1)}, bf16[512,128]{1,0:T(8,128)(2,1)}, u32[]{:S(2)}) copy-start(bf16[512,128]{1,0:T(8,128)(2,1)} %get-tuple-element.433) | copy-start | bytes 393220
  610.7 0.8 copy-start.1
Sparse Core Ops, SparseCore 0:
  10.8 134.4 all-gather.1
  162.5 64.1 all-reduce.1
where the time goes:
time: 621 us; the launch traced here: 618 us
  waiting for transfers between devices  229 us (37%)
  local copies, waits for them, and re-layouts  148 us (24%)
  blocking collectives  85 us (14%)
  matrix products  78 us (13%)
  other arithmetic  55.8 us (9%)
  between operations  13.6 us (2%)
  starting transfers between devices  7.75 us (1%)
    all_gather x1, waiting for transfers between devices, per_device(): lax.all_gather(alignment, 'row', axis=0, tiled=True)  138 us
    convert_element_type x12, local copies, waits for them, and re-layouts, forward_block(): outer.reshape(block_rows * cols_dev, FACTOR_CHANNELS * FACTOR_CHANNELS)  64.8 us
    psum x1, waiting for transfers between devices, from_root(): return lax.psum(jnp.where(mine, shard, jnp.zeros_like(shard)), axis)  62.7 us
    all_to_all x1, blocking collectives, mirrored(): lax.all_to_all(regrouped, 'row', split_axis=0, concat_axis=1, tiled=True)  50.7 us
    all_to_all x1, blocking collectives, mirrored(): lax.all_to_all(sectioned, 'col', split_axis=0, concat_axis=0, tiled=True)  34.3 us
    convert_element_type x6, local copies, waits for them, and re-layouts, per_device(): scores = own.astype(jnp.float32) + across.astype(jnp.float32)  27.8 us
    all_to_all x1, waiting for transfers between devices, mirrored(): lax.all_to_all(lax.all_to_all(regrouped, 'row', split_axis=0, concat_axis...  27.8 us
    dot_general x6, matrix products, backward_block(): jnp.dot(dhidden, w_expand.T, preferred_element_type=jnp.float32)  17.7 us
  transfers between devices with their start and end apart: 3, of which 3 were waited for; matrix products, arithmetic and copies ran while one was open for 2% of the time, Pallas kernels for 0%

commit v1 on v0

v1 whole, which is shorter than its diff:
```python
import functools

import jax
import jax.numpy as jnp
from jax import lax
from jax.experimental import pallas as pl
from jax.experimental.pallas import tpu as pltpu
from jax.sharding import PartitionSpec as P

MESH = pl.DeviceIdType.MESH
F32 = jnp.float32
BF16 = jnp.bfloat16
EPS = 1e-05
ROWS, COLS, CH = 48, 192, 128
HALF = 24
HID = 512


def dot(a, b):
    return lax.dot_general(a, b, (((1,), (0,)), ((), ())), preferred_element_type=F32)


def normalize(x):
    mean = jnp.mean(x, axis=-1, keepdims=True)
    centred = x - mean
    scale = lax.rsqrt(jnp.mean(centred * centred, axis=-1, keepdims=True) + EPS)
    return centred * scale, scale


def kernel(
    al, pair, t2, pw_right, place, w_outer_t, w_expand, w_shrink, bins2, shrink_t, expand_t, bins2_t,
    out,
    g_right, g_left, own_left, f_right, f_left, left_op, outer_op, middle, slope, logits, arrived, mirror,
    right_send, right_recv, left_send, left_recv, mir_send, mir_recv,
):
    r = lax.axis_index("row")
    c = lax.axis_index("col")
    z = lax.rem(r, 2)
    partner = r + 1 - 2 * z
    root = r // 4
    quarter = lax.rem(r, 4)

    bar = pltpu.get_barrier_semaphore()
    pl.semaphore_signal(bar, inc=1, device_id=(partner, c), device_id_type=MESH)

    def greet_plane(k, _):
        m = lax.rem(r // 2 + k, 16)
        pl.semaphore_signal(bar, inc=1, device_id=(2 * m + z, c), device_id_type=MESH)
        return 0

    lax.fori_loop(1, 16, greet_plane, 0)

    def greet_left(k, _):
        @pl.when(jnp.logical_or(k != r, root != c))
        def _():
            pl.semaphore_signal(bar, inc=1, device_id=(k, root), device_id_type=MESH)

        return 0

    lax.fori_loop(0, 32, greet_left, 0)
    for a in range(4):
        @pl.when(jnp.logical_or(4 * c + a != r, root != c))
        def _():
            pl.semaphore_signal(bar, inc=1, device_id=(4 * c + a, root), device_id_type=MESH)

    normed = []
    for s in range(2):
        normed.append(normalize(al[s].astype(F32))[0])
    tails = []
    for s in range(2):
        ft = lax.dot_general(
            pw_right[...], normed[s].astype(BF16), (((1,), (1,)), ((), ())), preferred_element_type=F32
        )
        g_right[r, pl.ds(32 * s, 32), :] = ft[:, :128].astype(BF16)
        tails.append(ft[:, 128:192])
    g_right[r, pl.ds(64, 32), :] = jnp.concatenate(tails, axis=1).astype(BF16)
    lf = None
    for h in range(2):
        for s in range(2):
            rows = jnp.concatenate(
                [normed[s][q * ROWS + h * HALF : q * ROWS + h * HALF + HALF] for q in range(4)], axis=0
            ).astype(BF16)
            term = dot(rows, place[2 * h + s])
            lf = term if lf is None else lf + term
    for q in range(4):
        own_left[q] = jnp.concatenate(
            [lf[q * HALF : (q + 1) * HALF], jnp.zeros((8, 128), F32)], axis=0
        ).astype(BF16)

    is_root = (root == c).astype(jnp.int32)
    pl.semaphore_wait(bar, 52 - 2 * is_root)

    def right_copy(block, slot, dest):
        return pltpu.make_async_remote_copy(
            src_ref=g_right.at[block], dst_ref=g_right.at[block],
            send_sem=right_send.at[slot], recv_sem=right_recv.at[block],
            device_id=(dest, c), device_id_type=MESH,
        )

    right_copy(r, 0, partner).start()

    def start_own(k, _):
        m = lax.rem(r // 2 + k, 16)
        right_copy(r, k, 2 * m + z).start()
        return 0

    lax.fori_loop(1, 16, start_own, 0)

    def left_copy(k):
        return pltpu.make_async_remote_copy(
            src_ref=own_left.at[k // 8], dst_ref=g_left.at[r],
            send_sem=left_send.at[k], recv_sem=left_recv.at[r],
            device_id=(4 * c + k // 8, lax.rem(k, 8)), device_id_type=MESH,
        )

    def left_self(k):
        return jnp.logical_and(4 * c + k // 8 == r, lax.rem(k, 8) == c)

    def start_left(k, _):
        mine = left_self(k)

        @pl.when(mine)
        def _():
            pltpu.make_async_copy(own_left.at[k // 8], g_left.at[r], left_recv.at[r]).start()

        @pl.when(jnp.logical_not(mine))
        def _():
            left_copy(k).start()

        return 0

    lax.fori_loop(0, 32, start_left, 0)

    right_copy(partner, 0, partner).wait_recv()

    def start_partner(k, _):
        m = lax.rem(r // 2 + k, 16)
        right_copy(partner, 15 + k, 2 * m + z).start()
        return 0

    lax.fori_loop(1, 16, start_partner, 0)

    def wait_left(k, _):
        pltpu.make_async_copy(g_left.at[k], g_left.at[k], left_recv.at[k]).wait()
        return 0

    lax.fori_loop(0, 32, wait_left, 0)

    def left_rows(k, _):
        f_left[pl.ds(pl.multiple_of(k * 32, 32), 32), :] = g_left[k].astype(F32) * (1.0 / 64.0)
        return 0

    lax.fori_loop(0, 32, left_rows, 0)

    def left_block(p, _):
        x = f_left[pl.ds(p, 32, stride=32), :]
        stack = jnp.concatenate([x] + [pltpu.roll(x, 128 - 32 * g, axis=1) for g in range(1, 4)], axis=0)
        left_op[pl.ds(pl.multiple_of(p * 32, 32), 32), :] = stack.T[:32].astype(BF16)
        return 0

    lax.fori_loop(0, HALF, left_block, 0)

    def wait_right(k, _):
        m = lax.rem(r // 2 + k, 16)
        right_copy(2 * m + z, 0, partner).wait_recv()
        right_copy(2 * m + 1 - z, 0, partner).wait_recv()
        return 0

    lax.fori_loop(1, 16, wait_right, 0)

    def right_rows(k, _):
        f_right[pl.ds(pl.multiple_of(k * 96, 96), 96), :] = g_right[k].astype(F32)
        return 0

    lax.fori_loop(0, 32, right_rows, 0)

    low = lax.broadcasted_iota(jnp.int32, (32, 128), 1) < 64

    def outer_step(e2, _):
        ab, tail = [], []
        zero = jnp.zeros((32, 128), F32)
        for par in range(2):
            e = 2 * e2 + par
            x0 = f_right[pl.ds(e, 32, stride=96), :]
            x1 = f_right[pl.ds(e + 32, 32, stride=96), :]
            xb = f_right[pl.ds(e + 64, 32, stride=96), :]
            xr = pltpu.roll(xb, 64, axis=1)
            h0 = jnp.concatenate([x0, x1, zero, zero], axis=0)
            h1 = jnp.concatenate([zero, zero, x0, x1], axis=0)
            ab.append(jnp.concatenate([h0, h1], axis=1).astype(BF16))
            tail.append(
                jnp.concatenate(
                    [
                        jnp.where(low, xb, zero), jnp.where(low, xr, zero),
                        jnp.where(low, zero, xr), jnp.where(low, zero, xb),
                    ],
                    axis=0,
                ).astype(BF16)
            )
        chunks = ab + [jnp.concatenate(tail, axis=1)]
        for which in range(3):
            for mb in range(6):
                res = dot(left_op[mb * 128 : (mb + 1) * 128, :], chunks[which]).astype(BF16)
                for pi in range(4):
                    p = mb * 4 + pi
                    piece = res[pi * 32 : (pi + 1) * 32]
                    if which < 2:
                        rows = pl.ds(pl.multiple_of((2 * e2 + which) * 32, 32), 32)
                        outer_op[p // 2, rows, pl.ds((p % 2) * 384, 256)] = piece
                    else:
                        for par in range(2):
                            rows = pl.ds(pl.multiple_of((2 * e2 + par) * 32, 32), 32)
                            outer_op[p // 2, rows, pl.ds((p % 2) * 384 + 256, 128)] = piece[
                                :, par * 128 : (par + 1) * 128
                            ]
        return 0

    lax.fori_loop(0, 16, outer_step, 0)

    def mirror_copy(st, a):
        return pltpu.make_async_remote_copy(
            src_ref=logits.at[pl.ds(2 * st, 2), pl.ds(a * ROWS, ROWS), :],
            dst_ref=arrived.at[quarter, pl.ds(2 * st, 2), :, :],
            send_sem=mir_send.at[st, a], recv_sem=mir_recv.at[st, quarter],
            device_id=(4 * c + a, root), device_id_type=MESH,
        )

    def mirror_is_self(a):
        return jnp.logical_and(4 * c + a == r, root == c)

    def forward_step(st, _):
        upd_t = dot(w_outer_t[...], outer_op[st])
        upd = [upd_t[:, k * 128 : (k + 1) * 128].T for k in range(6)]
        for t in range(2):
            p = 2 * st + t
            finals = []
            for h in range(2):
                i = p + HALF * h
                update = jnp.concatenate(
                    [upd[3 * t + h], upd[3 * t + 2][h * 64 : (h + 1) * 64]], axis=0
                )
                mid = (pair[i].astype(F32) + update).astype(BF16)
                middle[i] = mid
                mid = mid.astype(F32)
                xn = normalize(mid)[0].astype(BF16)
                before = dot(xn, w_expand[...]).astype(BF16).astype(F32)
                sig = 0.5 * jnp.tanh(0.5 * before) + 0.5
                hid = before * sig
                slope[i] = (sig + hid * (1.0 - sig)).astype(BF16)
                finals.append((mid + dot(hid.astype(BF16), w_shrink[...])).astype(BF16))
            logits[p] = dot(jnp.concatenate(finals, axis=1), bins2[...]).astype(BF16)
        for a in range(4):
            mine = mirror_is_self(a)

            @pl.when(mine)
            def _():
                pltpu.make_async_copy(
                    logits.at[pl.ds(2 * st, 2), pl.ds(a * ROWS, ROWS), :],
                    arrived.at[quarter, pl.ds(2 * st, 2), :, :],
                    mir_recv.at[st, quarter],
                ).start()

            @pl.when(jnp.logical_not(mine))
            def _():
                mirror_copy(st, a).start()

        return 0

    lax.fori_loop(0, 12, forward_step, 0)

    def take_mirror(st, _):
        for s in range(4):
            pltpu.make_async_copy(
                arrived.at[s, pl.ds(2 * st, 2), :, :], arrived.at[s, pl.ds(2 * st, 2), :, :], mir_recv.at[st, s]
            ).wait()
            for t in range(2):
                q = 2 * st + t
                rows = pl.ds(pl.multiple_of(s * 1152 + q * ROWS, 16), ROWS)
                mirror[rows, :] = arrived[s, q].astype(F32)
        return 0

    lax.fori_loop(0, 12, take_mirror, 0)

    lane = lax.broadcasted_iota(jnp.int32, (COLS, 128), 1)
    first = lane < 64
    code = lax.rem(lane, 64).astype(F32)
    sel_row = lax.broadcasted_iota(jnp.int32, (128, 128), 0)
    sel_half = HALF * (lax.broadcasted_iota(jnp.int32, (128, 128), 1) // 64)
    small = lax.broadcasted_iota(jnp.int32, (HALF, 128), 1) < 64

    def backward_step(p, _):
        parts = []
        for s in range(4):
            x0 = mirror[pl.ds(s * 1152 + p, HALF, stride=ROWS), :]
            x1 = mirror[pl.ds(s * 1152 + p + HALF, HALF, stride=ROWS), :]
            parts.append(jnp.where(small, x0, pltpu.roll(x1, 64, axis=1)))
            parts.append(jnp.where(small, pltpu.roll(x0, 64, axis=1), x1))
        scores = logits[p].astype(F32) + jnp.concatenate(parts, axis=0)
        low_max = jnp.max(jnp.where(first, scores, -jnp.inf), axis=-1, keepdims=True)
        high_max = jnp.max(jnp.where(first, -jnp.inf, scores), axis=-1, keepdims=True)
        expo = jnp.exp(scores - jnp.where(first, low_max, high_max))
        low_sum = jnp.sum(jnp.where(first, expo, 0.0), axis=-1, keepdims=True)
        high_sum = jnp.sum(jnp.where(first, 0.0, expo), axis=-1, keepdims=True)
        prob = expo * jnp.where(first, 1.0 / low_sum, 1.0 / high_sum)
        pick_t = (sel_row == sel_half + p).astype(BF16)
        pick_w = (sel_row == sel_half + (p + 64)).astype(BF16)
        goal = dot(t2[...], pick_t)
        weight = dot(t2[...], pick_w)
        dlog = ((prob - jnp.where(goal == code, 1.0, 0.0)) * weight).astype(BF16)
        dfin = dot(dlog, bins2_t[...])
        for h in range(2):
            i = p + HALF * h
            grad = dfin[:, h * 128 : (h + 1) * 128]
            dh = (dot(grad.astype(BF16), shrink_t[...]) * slope[i].astype(F32)).astype(BF16)
            dxn = dot(dh, expand_t[...])
            xhat, scale = normalize(middle[i].astype(F32))
            g1 = jnp.mean(dxn, axis=-1, keepdims=True)
            g2 = jnp.mean(dxn * xhat, axis=-1, keepdims=True)
            out[i] = (grad + scale * (dxn - g1 - xhat * g2)).astype(BF16)
        return 0

    lax.fori_loop(0, HALF, backward_step, 0)

    def drain_right(k, _):
        right_copy(r, k, partner).wait_send()
        return 0

    lax.fori_loop(0, 31, drain_right, 0)

    def drain_left(k, _):
        @pl.when(jnp.logical_not(left_self(k)))
        def _():
            left_copy(k).wait_send()

        return 0

    lax.fori_loop(0, 32, drain_left, 0)

    def drain_mirror(st, _):
        for a in range(4):
            @pl.when(jnp.logical_not(mirror_is_self(a)))
            def _():
                mirror_copy(st, a).wait_send()

        return 0

    lax.fori_loop(0, 12, drain_mirror, 0)


def per_device(
    alignment, pair_act, targets, crop_mask, projection_weight, w_outer, w_expand, w_shrink, w_bins
):
    row = lax.axis_index("row")
    col = lax.axis_index("col")
    row_mask = lax.dynamic_slice_in_dim(crop_mask, row * ROWS, ROWS)
    col_mask = lax.dynamic_slice_in_dim(crop_mask, col * COLS, COLS)
    weight = 2 * col_mask[:, None] * row_mask[None, :]
    pad = jnp.zeros((COLS, 16), jnp.int32)
    t2 = jnp.concatenate([targets.T, pad, weight, pad], axis=1).astype(BF16)
    pw_right = projection_weight[:, 32:].T
    left_w = projection_weight[:, :32]
    place = jnp.stack([jnp.pad(left_w, ((0, 0), (32 * g, 96 - 32 * g))) for g in range(4)])
    w_outer_t = w_outer.reshape(32, 32, CH).transpose(2, 1, 0).reshape(CH, 1024)
    zero = jnp.zeros_like(w_bins)
    bins2 = jnp.concatenate(
        [jnp.concatenate([w_bins, zero], axis=1), jnp.concatenate([zero, w_bins], axis=1)], axis=0
    )
    vmem = pl.BlockSpec(memory_space=pltpu.VMEM)
    return pl.pallas_call(
        kernel,
        out_shape=jax.ShapeDtypeStruct((ROWS, COLS, CH), BF16),
        in_specs=[vmem] * 12,
        out_specs=vmem,
        scratch_shapes=[
            pltpu.VMEM((32, 96, 128), BF16),
            pltpu.VMEM((32, 32, 128), BF16),
            pltpu.VMEM((4, 32, 128), BF16),
            pltpu.VMEM((3072, 128), F32),
            pltpu.VMEM((1024, 128), F32),
            pltpu.VMEM((768, 128), BF16),
            pltpu.VMEM((12, 1024, 768), BF16),
            pltpu.VMEM((ROWS, COLS, CH), BF16),
            pltpu.VMEM((ROWS, COLS, HID), BF16),
            pltpu.VMEM((HALF, COLS, 128), BF16),
            pltpu.VMEM((4, HALF, ROWS, 128), BF16),
            pltpu.VMEM((4 * HALF * ROWS, 128), F32),
            pltpu.SemaphoreType.DMA((31,)),
            pltpu.SemaphoreType.DMA((32,)),
            pltpu.SemaphoreType.DMA((32,)),
            pltpu.SemaphoreType.DMA((32,)),
            pltpu.SemaphoreType.DMA((12, 4)),
            pltpu.SemaphoreType.DMA((12, 4)),
        ],
        compiler_params=pltpu.CompilerParams(
            collective_id=0, has_side_effects=True, vmem_limit_bytes=63 * 1024 * 1024
        ),
    )(
        alignment, pair_act, t2, pw_right, place, w_outer_t, w_expand, w_shrink, bins2,
        w_shrink.T, w_expand.T, bins2.T,
    )


def solution(mesh):
    in_specs = (
        P("row", "col", None), P("row", "col", None), P("row", "col"),
        P(), P(), P(), P(), P(), P(),
    )
    return jax.shard_map(
        per_device, mesh=mesh, in_specs=in_specs, out_specs=P("row", "col", None), check_vma=False
    )
```

time: 621 us -> 146 us (0.24)
  waiting for transfers between devices: 229 us -> 0 us
  local copies, waits for them, and re-layouts: 148 us -> 10.7 us
  Pallas kernels: 0 us -> 130 us
  blocking collectives: 85 us -> 0 us
  matrix products: 78 us -> 0 us
  other arithmetic: 55.8 us -> 4.55 us
  between operations: 13.6 us -> 0.04 us
  starting transfers between devices: 7.75 us -> 0 us
    all_gather x1 -> x0, waiting for transfers between devices: 138 us -> none  [per_device(): lax.all_gather(alignment, 'row', axis=0, tiled=True)]
    pallas_call x0 -> x1, Pallas kernels: none -> 130 us  [per_device(): pl.pallas_call(kernel, out_shape=jax.ShapeDtypeStruct((ROWS, COLS, CH), B...]
    convert_element_type x30 -> x0, local copies, waits for them, and re-layouts: 108 us -> none  [the longest x12 64.8 us: forward_block(): outer.reshape(block_rows * cols_dev, FACTOR_CHANNELS * FACTOR_CHANNELS)]
    all_to_all x2 -> x0, blocking collectives: 85 us -> none  [the longest x1 50.7 us: mirrored(): lax.all_to_all(regrouped, 'row', split_axis=0, concat_axis=1, tiled=True)]
    dot_general x37 -> x0, matrix products: 78 us -> none  [the longest x6 17.7 us: backward_block(): jnp.dot(dhidden, w_expand.T, preferred_element_type=jnp.float32)]
    psum x1 -> x0, waiting for transfers between devices: 62.7 us -> none  [from_root(): return lax.psum(jnp.where(mine, shard, jnp.zeros_like(shard)), axis)]
    all_to_all x1 -> x0, waiting for transfers between devices: 27.8 us -> none  [mirrored(): lax.all_to_all(lax.all_to_all(regrouped, 'row', split_axis=0, concat_axis...]
    reduce_sum x33 -> x0, other arithmetic: 23.7 us -> none  [the longest x13 8.13 us: layer_normalize(): jnp.mean(centred * centred, axis=-1, keepdims=True) + epsilon]
  transfers between devices with their start and end apart: 3 -> 0, of which waited for: 3 -> 0; matrix products, arithmetic and copies ran while one was open for 2% -> 0% of each run, Pallas kernels for 0% -> 0%
where the time goes in v1:
time: 146 us; the launch traced here: 145 us
  Pallas kernels  130 us (89%)
  local copies, waits for them, and re-layouts  10.7 us (7%)
  other arithmetic  4.55 us (3%)
    pallas_call x1, Pallas kernels, per_device(): pl.pallas_call(kernel, out_shape=jax.ShapeDtypeStruct((ROWS, COLS, CH), B...  130 us
    unnamed x6, local copies, waits for them, and re-layouts  6.66 us

profile of v1, /device:TPU:1, one launch (start us, length us, event | category | flops | bytes accessed | tf_op | source)
XLA Modules:
  0.0 145.0 jit_solution(2637163779262767192)
XLA Ops:
  0.0 0.0 copy-start
  0.0 0.8 dynamic_slice.7
  0.8 0.8 dynamic-slice_multiply_fusion
  1.6 0.8 convert.11
  2.4 0.1 copy.29
  2.5 1.3 fusion.4
  3.8 0.1 multiply_convert_fusion
  3.9 0.1 copy.36
  4.1 0.7 pad_maximum_fusion.1.t2
  4.8 1.7 %copy.33 = bf16[128,512]{0,1:T(8,128)(2,1)} copy(bf16[128,512]{1,0:T(8,128)(2,1)} %w_expand.1) | data formatting | bytes 262144 | tf_op args[6]
  6.5 1.7 %copy.32 = bf16[512,128]{0,1:T(8,128)(2,1)} copy(bf16[512,128]{1,0:T(8,128)(2,1)} %w_shrink.1) | data formatting | bytes 262144 | tf_op args[7]
  8.1 1.4 fusion.3
  9.5 0.7 copy.35.bins2
  10.3 0.1 pad_bitcast_fusion.3
  10.4 0.7 pad_maximum_fusion.place
  11.1 0.0 copy-done
  11.1 0.1 copy.31
  11.2 0.8 copy.34.w_outer_t
  12.1 129.6 %shard_map.91 = bf16[48,192,128]{2,1,0:T(8,128)(2,1)} custom-call(bf16[2,192,256]{2,1,0:T(8,128)(2,1)} %al.1, bf16[48,192,128]{2,1,0:T(8,128)(2,1)} %pair.1, bf16[192,128]{1,0:T(8,128)(2,1)} %pad_maximum_fusion.1.t2, bf16[32,256]{1,0:T(8,128)(2,1)} %get-tuple-element.10.pw_right, bf16[4,256,128]{2,1,0:T(8,128)(2,1)} %pad_maximum_fusion.place, ...), custom_call_target="tpu_custom_call" | custom-call | tf_op jit(solution)/shard_map/pallas_call | solution.py:369
  141.7 3.2 %copy.38 = bf16[48,192,128]{2,1,0:T(8,128)(2,1)} copy(bf16[48,192,128]{2,1,0:T(8,128)(2,1)} %shard_map.91) | data formatting | bytes 4718592
  (1 shorter events, 0.0 us)
Async XLA Ops:
  0.0 11.1 %copy-start = (bf16[1024,128]{1,0:T(8,128)(2,1)S(1)}, bf16[1024,128]{1,0:T(8,128)(2,1)}, u32[]{:S(2)}) copy-start(bf16[1024,128]{1,0:T(8,128)(2,1)} %param.14) | copy-start | bytes 786436

commit v2 on v1

--- a/solution.py
+++ b/solution.py
@@ -14,6 +14,9 @@
 ROWS, COLS, CH = 48, 192, 128
 HALF = 24
 HID = 512
+OUTER_BLOCKS = 1
+BACK_ROWS = 2
+FORWARD_GROUP = 4
 
 
 def dot(a, b):
@@ -28,10 +31,11 @@
 
 
 def kernel(
-    al, pair, t2, pw_right, place, w_outer_t, w_expand, w_shrink, bins2, shrink_t, expand_t, bins2_t,
+    al, pair, targets, mask_rows, mask, pw, w_outer, w_expand, w_shrink, w_bins,
     out,
     g_right, g_left, own_left, f_right, f_left, left_op, outer_op, middle, slope, logits, arrived, mirror,
-    right_send, right_recv, left_send, left_recv, mir_send, mir_recv,
+    relay, w_outer_t, half_expand, bins2, half_shrink_t, expand_t, bins2_t, goals,
+    right_send, right_recv, left_send, left_recv, mir_send, mir_recv, relay_send, relay_recv, pass_send,
 ):
     r = lax.axis_index("row")
     c = lax.axis_index("col")
@@ -39,6 +43,10 @@
     partner = r + 1 - 2 * z
     root = r // 4
     quarter = lax.rem(r, 4)
+    y = r // 8
+    diagonal = y == c // 2
+    off_diagonal = jnp.logical_not(diagonal)
+    in_plane = lax.rem(r, 8)
 
     bar = pltpu.get_barrier_semaphore()
     pl.semaphore_signal(bar, inc=1, device_id=(partner, c), device_id_type=MESH)
@@ -62,6 +70,24 @@
         @pl.when(jnp.logical_or(4 * c + a != r, root != c))
         def _():
             pl.semaphore_signal(bar, inc=1, device_id=(4 * c + a, root), device_id_type=MESH)
+
+    @pl.when(off_diagonal)
+    def _():
+        for s in range(4):
+            pl.semaphore_signal(
+                bar, inc=1, device_id=(8 * y + lax.rem(4 * c + s, 8), root), device_id_type=MESH
+            )
+
+    @pl.when(diagonal)
+    def _():
+        for k in range(1, 4):
+            pl.semaphore_signal(
+                bar, inc=1, device_id=(8 * lax.rem(y + k, 4) + in_plane, c), device_id_type=MESH
+            )
+
+    pw_pad = jnp.concatenate([pw[...].astype(F32), jnp.zeros((256, 64), F32)], axis=1)
+    pw_right = pw_pad.T[32:64].astype(BF16)
+    pw_left = jnp.where(lax.broadcasted_iota(jnp.int32, (256, 128), 1) < 32, pw_pad, 0.0)
 
     normed = []
     for s in range(2):
@@ -69,7 +95,7 @@
     tails = []
     for s in range(2):
         ft = lax.dot_general(
-            pw_right[...], normed[s].astype(BF16), (((1,), (1,)), ((), ())), preferred_element_type=F32
+            pw_right, normed[s].astype(BF16), (((1,), (1,)), ((), ())), preferred_element_type=F32
         )
         g_right[r, pl.ds(32 * s, 32), :] = ft[:, :128].astype(BF16)
         tails.append(ft[:, 128:192])
@@ -80,7 +106,9 @@
             rows = jnp.concatenate(
                 [normed[s][q * ROWS + h * HALF : q * ROWS + h * HALF + HALF] for q in range(4)], axis=0
             ).astype(BF16)
-            term = dot(rows, place[2 * h + s])
+            shift = 32 * (2 * h + s)
+            place = pltpu.roll(pw_left, shift, axis=1) if shift else pw_left
+            term = dot(rows, place.astype(BF16))
             lf = term if lf is None else lf + term
     for q in range(4):
         own_left[q] = jnp.concatenate(
@@ -88,7 +116,8 @@
         ).astype(BF16)
 
     is_root = (root == c).astype(jnp.int32)
-    pl.semaphore_wait(bar, 52 - 2 * is_root)
+    on_diagonal = diagonal.astype(jnp.int32)
+    pl.semaphore_wait(bar, 53 - 2 * is_root + 11 * on_diagonal)
 
     def right_copy(block, slot, dest):
         return pltpu.make_async_remote_copy(
@@ -130,6 +159,32 @@
         return 0
 
     lax.fori_loop(0, 32, start_left, 0)
+
+    for k in range(4):
+        cols = slice(k * 128, (k + 1) * 128)
+        half_shrink_t[:, cols] = (0.5 * w_shrink[cols, :].astype(F32)).T.astype(BF16)
+        expand_t[cols, :] = w_expand[:, cols].astype(F32).T.astype(BF16)
+    half_expand[...] = (0.5 * w_expand[...].astype(F32)).astype(BF16)
+    wb = jnp.concatenate([w_bins[...].astype(F32), jnp.zeros((128, 64), F32)], axis=1)
+    wb_high = pltpu.roll(wb, 64, axis=1)
+    bins2[0:128, :] = wb.astype(BF16)
+    bins2[128:256, :] = wb_high.astype(BF16)
+    bins2_t[:, 0:128] = wb.T.astype(BF16)
+    bins2_t[:, 128:256] = wb_high.T.astype(BF16)
+    mirror[0:1024, :] = w_outer[...].astype(F32)
+    for k in range(8):
+        block = jnp.concatenate([mirror[pl.ds(4 * k + e, 32, stride=32), :] for e in range(4)], axis=0)
+        w_outer_t[:, k * 128 : (k + 1) * 128] = block.T.astype(BF16)
+    table = jnp.concatenate(
+        [
+            targets[...].astype(F32),
+            2.0 * mask_rows[pl.ds(c, 1), :].astype(F32),
+            jnp.zeros((79, COLS), F32),
+        ],
+        axis=0,
+    )
+    table = jnp.concatenate([table, jnp.zeros((128, 64), F32)], axis=1)
+    goals[...] = jnp.concatenate([table[:, :128].T, table[:, 128:].T[:64]], axis=0).astype(BF16)
 
     right_copy(partner, 0, partner).wait_recv()
 
@@ -199,10 +254,11 @@
             )
         chunks = ab + [jnp.concatenate(tail, axis=1)]
         for which in range(3):
-            for mb in range(6):
-                res = dot(left_op[mb * 128 : (mb + 1) * 128, :], chunks[which]).astype(BF16)
-                for pi in range(4):
-                    p = mb * 4 + pi
+            for mb in range(OUTER_BLOCKS):
+                span = 768 // OUTER_BLOCKS
+                res = dot(left_op[mb * span : (mb + 1) * span, :], chunks[which]).astype(BF16)
+                for pi in range(span // 32):
+                    p = mb * (span // 32) + pi
                     piece = res[pi * 32 : (pi + 1) * 32]
                     if which < 2:
                         rows = pl.ds(pl.multiple_of((2 * e2 + which) * 32, 32), 32)
@@ -228,41 +284,84 @@
     def mirror_is_self(a):
         return jnp.logical_and(4 * c + a == r, root == c)
 
+    def relay_copy(b):
+        return pltpu.make_async_remote_copy(
+            src_ref=logits.at[pl.ds(4 * b, 2), :, :], dst_ref=relay.at[y, b],
+            send_sem=relay_send.at[b], recv_sem=relay_recv.at[y, b],
+            device_id=(8 * (c // 2) + in_plane, c), device_id_type=MESH,
+        )
+
+    def pass_copy(source, b, a):
+        return pltpu.make_async_remote_copy(
+            src_ref=relay.at[source, b, :, pl.ds(a * ROWS, ROWS), :],
+            dst_ref=arrived.at[quarter, pl.ds(4 * b, 2), :, :],
+            send_sem=pass_send.at[source, b, a], recv_sem=mir_recv.at[2 * b, quarter],
+            device_id=(4 * c + a, 2 * source + in_plane // 4), device_id_type=MESH,
+        )
+
+    def is_relayed(st):
+        return jnp.logical_and(jnp.logical_and(off_diagonal, lax.rem(st, 2) == 0), st < 10)
+
     def forward_step(st, _):
         upd_t = dot(w_outer_t[...], outer_op[st])
         upd = [upd_t[:, k * 128 : (k + 1) * 128].T for k in range(6)]
+        order = [(t, h) for t in range(2) for h in range(2)]
+        finals = []
+        for g in range(0, 4, FORWARD_GROUP):
+            group = order[g : g + FORWARD_GROUP]
+            ids = [2 * st + t + HALF * h for t, h in group]
+            update = jnp.concatenate(
+                [x for t, h in group for x in (upd[3 * t + h], upd[3 * t + 2][h * 64 : (h + 1) * 64])], axis=0
+            )
+            mid = (jnp.concatenate([pair[i] for i in ids], axis=0).astype(F32) + update).astype(BF16)
+            for n, i in enumerate(ids):
+                middle[i] = mid[n * COLS : (n + 1) * COLS]
+            mid = mid.astype(F32)
+            xn = normalize(mid)[0].astype(BF16)
+            half = dot(xn, half_expand[...]).astype(BF16).astype(F32)
+            th = jnp.tanh(half)
+            hid = half + half * th
+            slopes = ((1.0 + th) + (hid - hid * th)).astype(BF16)
+            for n, i in enumerate(ids):
+                slope[i] = slopes[n * COLS : (n + 1) * COLS]
+            final = (mid + dot(hid.astype(BF16), w_shrink[...])).astype(BF16)
+            finals += [final[n * COLS : (n + 1) * COLS] for n in range(FORWARD_GROUP)]
+        wide = jnp.concatenate(
+            [jnp.concatenate(finals[0:2], axis=1), jnp.concatenate(finals[2:4], axis=1)], axis=0
+        )
+        logit = dot(wide, bins2[...]).astype(BF16)
         for t in range(2):
-            p = 2 * st + t
-            finals = []
-            for h in range(2):
-                i = p + HALF * h
-                update = jnp.concatenate(
-                    [upd[3 * t + h], upd[3 * t + 2][h * 64 : (h + 1) * 64]], axis=0
-                )
-                mid = (pair[i].astype(F32) + update).astype(BF16)
-                middle[i] = mid
-                mid = mid.astype(F32)
-                xn = normalize(mid)[0].astype(BF16)
-                before = dot(xn, w_expand[...]).astype(BF16).astype(F32)
-                sig = 0.5 * jnp.tanh(0.5 * before) + 0.5
-                hid = before * sig
-                slope[i] = (sig + hid * (1.0 - sig)).astype(BF16)
-                finals.append((mid + dot(hid.astype(BF16), w_shrink[...])).astype(BF16))
-            logits[p] = dot(jnp.concatenate(finals, axis=1), bins2[...]).astype(BF16)
-        for a in range(4):
-            mine = mirror_is_self(a)
-
-            @pl.when(mine)
-            def _():
-                pltpu.make_async_copy(
-                    logits.at[pl.ds(2 * st, 2), pl.ds(a * ROWS, ROWS), :],
-                    arrived.at[quarter, pl.ds(2 * st, 2), :, :],
-                    mir_recv.at[st, quarter],
-                ).start()
-
-            @pl.when(jnp.logical_not(mine))
-            def _():
-                mirror_copy(st, a).start()
+            logits[2 * st + t] = logit[t * COLS : (t + 1) * COLS]
+
+        @pl.when(is_relayed(st))
+        def _():
+            relay_copy(st // 2).start()
+
+        @pl.when(jnp.logical_not(is_relayed(st)))
+        def _():
+            for a in range(4):
+                mine = mirror_is_self(a)
+
+                @pl.when(mine)
+                def _():
+                    pltpu.make_async_copy(
+                        logits.at[pl.ds(2 * st, 2), pl.ds(a * ROWS, ROWS), :],
+                        arrived.at[quarter, pl.ds(2 * st, 2), :, :],
+                        mir_recv.at[st, quarter],
+                    ).start()
+
+                @pl.when(jnp.logical_not(mine))
+                def _():
+                    mirror_copy(st, a).start()
+
+        @pl.when(jnp.logical_and(diagonal, jnp.logical_and(lax.rem(st, 2) == 1, st > 1)))
+        def _():
+            b = (st - 3) // 2
+            for k in range(1, 4):
+                source = lax.rem(y + k, 4)
+                pltpu.make_async_copy(relay.at[source, b], relay.at[source, b], relay_recv.at[source, b]).wait()
+                for a in range(4):
+                    pass_copy(source, b, a).start()
 
         return 0
 
@@ -288,7 +387,9 @@
     sel_half = HALF * (lax.broadcasted_iota(jnp.int32, (128, 128), 1) // 64)
     small = lax.broadcasted_iota(jnp.int32, (HALF, 128), 1) < 64
 
-    def backward_step(p, _):
+    col_weight = jnp.broadcast_to(goals[:, 48:49].astype(F32), (COLS, 128))
+
+    def backward_row(p):
         parts = []
         for s in range(4):
             x0 = mirror[pl.ds(s * 1152 + p, HALF, stride=ROWS), :]
@@ -302,24 +403,30 @@
         low_sum = jnp.sum(jnp.where(first, expo, 0.0), axis=-1, keepdims=True)
         high_sum = jnp.sum(jnp.where(first, 0.0, expo), axis=-1, keepdims=True)
         prob = expo * jnp.where(first, 1.0 / low_sum, 1.0 / high_sum)
-        pick_t = (sel_row == sel_half + p).astype(BF16)
-        pick_w = (sel_row == sel_half + (p + 64)).astype(BF16)
-        goal = dot(t2[...], pick_t)
-        weight = dot(t2[...], pick_w)
+        goal = dot(goals[...], (sel_row == sel_half + p).astype(BF16))
+        m0 = mask[r * ROWS + p].astype(F32)
+        m1 = mask[r * ROWS + p + HALF].astype(F32)
+        weight = col_weight * jnp.where(first, m0, m1)
         dlog = ((prob - jnp.where(goal == code, 1.0, 0.0)) * weight).astype(BF16)
         dfin = dot(dlog, bins2_t[...])
-        for h in range(2):
-            i = p + HALF * h
-            grad = dfin[:, h * 128 : (h + 1) * 128]
-            dh = (dot(grad.astype(BF16), shrink_t[...]) * slope[i].astype(F32)).astype(BF16)
-            dxn = dot(dh, expand_t[...])
-            xhat, scale = normalize(middle[i].astype(F32))
-            g1 = jnp.mean(dxn, axis=-1, keepdims=True)
-            g2 = jnp.mean(dxn * xhat, axis=-1, keepdims=True)
-            out[i] = (grad + scale * (dxn - g1 - xhat * g2)).astype(BF16)
-        return 0
-
-    lax.fori_loop(0, HALF, backward_step, 0)
+        grad = jnp.concatenate([dfin[:, :128], dfin[:, 128:]], axis=0)
+        slopes = jnp.concatenate([slope[p], slope[p + HALF]], axis=0)
+        dh = (dot(grad.astype(BF16), half_shrink_t[...]) * slopes.astype(F32)).astype(BF16)
+        dxn = dot(dh, expand_t[...])
+        mid = jnp.concatenate([middle[p], middle[p + HALF]], axis=0)
+        xhat, scale = normalize(mid.astype(F32))
+        g1 = jnp.mean(dxn, axis=-1, keepdims=True)
+        g2 = jnp.mean(dxn * xhat, axis=-1, keepdims=True)
+        res = (grad + scale * (dxn - g1 - xhat * g2)).astype(BF16)
+        out[p] = res[:COLS]
+        out[p + HALF] = res[COLS:]
+
+    def backward_step(k, _):
+        for t in range(BACK_ROWS):
+            backward_row(BACK_ROWS * k + t)
+        return 0
+
+    lax.fori_loop(0, HALF // BACK_ROWS, backward_step, 0)
 
     def drain_right(k, _):
         right_copy(r, k, partner).wait_send()
@@ -337,39 +444,40 @@
     lax.fori_loop(0, 32, drain_left, 0)
 
     def drain_mirror(st, _):
-        for a in range(4):
-            @pl.when(jnp.logical_not(mirror_is_self(a)))
-            def _():
-                mirror_copy(st, a).wait_send()
+        @pl.when(is_relayed(st))
+        def _():
+            relay_copy(st // 2).wait_send()
+
+        @pl.when(jnp.logical_not(is_relayed(st)))
+        def _():
+            for a in range(4):
+                @pl.when(jnp.logical_not(mirror_is_self(a)))
+                def _():
+                    mirror_copy(st, a).wait_send()
 
         return 0
 
     lax.fori_loop(0, 12, drain_mirror, 0)
+
+    @pl.when(diagonal)
+    def _():
+        def drain_pass(b, _):
+            for k in range(1, 4):
+                for a in range(4):
+                    pass_copy(lax.rem(y + k, 4), b, a).wait_send()
+            return 0
+
+        lax.fori_loop(0, 5, drain_pass, 0)
 
 
 def per_device(
     alignment, pair_act, targets, crop_mask, projection_weight, w_outer, w_expand, w_shrink, w_bins
 ):
-    row = lax.axis_index("row")
-    col = lax.axis_index("col")
-    row_mask = lax.dynamic_slice_in_dim(crop_mask, row * ROWS, ROWS)
-    col_mask = lax.dynamic_slice_in_dim(crop_mask, col * COLS, COLS)
-    weight = 2 * col_mask[:, None] * row_mask[None, :]
-    pad = jnp.zeros((COLS, 16), jnp.int32)
-    t2 = jnp.concatenate([targets.T, pad, weight, pad], axis=1).astype(BF16)
-    pw_right = projection_weight[:, 32:].T
-    left_w = projection_weight[:, :32]
-    place = jnp.stack([jnp.pad(left_w, ((0, 0), (32 * g, 96 - 32 * g))) for g in range(4)])
-    w_outer_t = w_outer.reshape(32, 32, CH).transpose(2, 1, 0).reshape(CH, 1024)
-    zero = jnp.zeros_like(w_bins)
-    bins2 = jnp.concatenate(
-        [jnp.concatenate([w_bins, zero], axis=1), jnp.concatenate([zero, w_bins], axis=1)], axis=0
-    )
     vmem = pl.BlockSpec(memory_space=pltpu.VMEM)
     return pl.pallas_call(
         kernel,
         out_shape=jax.ShapeDtypeStruct((ROWS, COLS, CH), BF16),
-        in_specs=[vmem] * 12,
+        in_specs=[vmem] * 4 + [pl.BlockSpec(memory_space=pltpu.SMEM)] + [vmem] * 5,
         out_specs=vmem,
         scratch_shapes=[
             pltpu.VMEM((32, 96, 128), BF16),
@@ -384,19 +492,30 @@
             pltpu.VMEM((HALF, COLS, 128), BF16),
             pltpu.VMEM((4, HALF, ROWS, 128), BF16),
             pltpu.VMEM((4 * HALF * ROWS, 128), F32),
+            pltpu.VMEM((4, 5, 2, COLS, 128), BF16),
+            pltpu.VMEM((128, 1024), BF16),
+            pltpu.VMEM((128, HID), BF16),
+            pltpu.VMEM((256, 128), BF16),
+            pltpu.VMEM((128, HID), BF16),
+            pltpu.VMEM((HID, 128), BF16),
+            pltpu.VMEM((128, 256), BF16),
+            pltpu.VMEM((COLS, 128), BF16),
             pltpu.SemaphoreType.DMA((31,)),
             pltpu.SemaphoreType.DMA((32,)),
             pltpu.SemaphoreType.DMA((32,)),
             pltpu.SemaphoreType.DMA((32,)),
             pltpu.SemaphoreType.DMA((12, 4)),
             pltpu.SemaphoreType.DMA((12, 4)),
+            pltpu.SemaphoreType.DMA((5,)),
+            pltpu.SemaphoreType.DMA((4, 5)),
+            pltpu.SemaphoreType.DMA((4, 5, 4)),
         ],
         compiler_params=pltpu.CompilerParams(
             collective_id=0, has_side_effects=True, vmem_limit_bytes=63 * 1024 * 1024
         ),
     )(
-        alignment, pair_act, t2, pw_right, place, w_outer_t, w_expand, w_shrink, bins2,
-        w_shrink.T, w_expand.T, bins2.T,
+        alignment, pair_act, targets, crop_mask.reshape(8, COLS), crop_mask, projection_weight,
+        w_outer, w_expand, w_shrink, w_bins,
     )
 
 

time: 146 us -> 108 us (0.74)
  Pallas kernels: 130 us -> 100 us
  other arithmetic: 4.55 us -> 0 us
  local copies, waits for them, and re-layouts: 10.7 us -> 7.49 us
    pallas_call x1, Pallas kernels: 130 us -> 100 us  [per_device(): pl.pallas_call(kernel, out_shape=jax.ShapeDtypeStruct((ROWS, COLS, CH), B...]
    another operation x3 -> x0, other arithmetic: 1.63 us -> none
    unnamed x6 -> x3, local copies, waits for them, and re-layouts: 6.66 us -> 6.13 us
where the time goes in v2:
time: 108 us
  Pallas kernels  100 us (93%)
  local copies, waits for them, and re-layouts  7.49 us (7%)
    pallas_call x1, Pallas kernels, per_device(): pl.pallas_call(kernel, out_shape=jax.ShapeDtypeStruct((ROWS, COLS, CH), B...  100 us
    unnamed x3, local copies, waits for them, and re-layouts  6.13 us

profile of v2, /device:TPU:1, one launch (start us, length us, event | category | flops | bytes accessed | tf_op | source)
XLA Modules:
  0.0 108.0 jit_solution(9583421754452265934)
XLA Ops:
  0.0 1.4 %reshape.3.mask_rows = s32[8,192]{1,0:T(8,128)} reshape(s32[1536]{0:T(1024)} %mask.1) | data formatting | bytes 12288 | tf_op jit(solution)/shard_map/reshape | solution.py:517
  1.4 1.4 %copy.11.w_bins = bf16[128,64]{1,0:T(8,128)(2,1)} copy(bf16[128,64]{0,1:T(8,128)(2,1)} %param.17) | data formatting | bytes 32768 | tf_op args[8]
  2.8 1.5 %copy.10.pw = bf16[256,64]{1,0:T(8,128)(2,1)} copy(bf16[256,64]{0,1:T(8,128)(2,1)} %param.13) | data formatting | bytes 65536 | tf_op args[4]
  4.3 100.4 %shard_map.91 = bf16[48,192,128]{2,1,0:T(8,128)(2,1)} custom-call(bf16[2,192,256]{2,1,0:T(8,128)(2,1)} %al.1, bf16[48,192,128]{2,1,0:T(8,128)(2,1)} %pair.1, s32[48,192]{1,0:T(8,128)} %targets.1, s32[8,192]{1,0:T(8,128)} %reshape.3.mask_rows, s32[1536]{0:T(1024)} %mask.1, bf16[256,64]{1,0:T(8,128)(2,1)} %copy.10.pw, bf16[1024,128]{1,0:T(8,128)(2,1)} %w_outer.1, ...), custom_call_target="tpu_custom_call" | custom-call | tf_op jit(solution)/shard_map/pallas_call | solution.py:477
  104.7 3.2 %copy.13 = bf16[48,192,128]{2,1,0:T(8,128)(2,1)} copy(bf16[48,192,128]{2,1,0:T(8,128)(2,1)} %shard_map.91) | data formatting | bytes 4718592

commit v3 on v2

v3 whole, which is shorter than its diff:
```python
import functools

import jax
import jax.numpy as jnp
from jax import lax
from jax.experimental import pallas as pl
from jax.experimental.pallas import tpu as pltpu
from jax.sharding import PartitionSpec as P

MESH = pl.DeviceIdType.MESH
F32 = jnp.float32
BF16 = jnp.bfloat16
EPS = 1e-05
ROWS, COLS, CH = 48, 192, 128
HALF = 24
HID = 512
OUTER_BLOCKS = 1
FORWARD_GROUP = 4
BACK_ROWS = 8
CHUNK = 64
EMIT_ROWS = 12
RELAYED = 6
LAG = 2
OUTER_UNROLL = 2
BACK_UNROLL = 1
ORDER = [a * 6 + h * 3 + k for k in range(3) for a in range(4) for h in range(2)]
BACK_ORDER = [ORDER.index(n) for n in range(24)]


def dot(a, b):
    return lax.dot_general(a, b, (((1,), (0,)), ((), ())), preferred_element_type=F32)


def permute(x, order):
    return jnp.concatenate([x[8 * n : 8 * n + 8] for n in order], axis=0)


def normalize(x):
    mean = jnp.mean(x, axis=-1, keepdims=True)
    centred = x - mean
    scale = lax.rsqrt(jnp.mean(centred * centred, axis=-1, keepdims=True) + EPS)
    return centred * scale, scale


def kernel(
    al, pair, targets, mask_rows, mask, pw_t, w_outer, w_expand, w_shrink, w_bins_t,
    out,
    g_right, g_left, own_left, f_right, f_left, left_op, right_op, outer_op, middle, slope, logits, arrived, mirror,
    relay, w_outer_t, half_expand, bins2, half_shrink_t, expand_t, bins2_t, goals, upd_even, upd_odd,
    right_send, right_recv, left_send, left_recv, mir_send, mir_recv, relay_send, relay_recv, pass_send,
):
    r = lax.axis_index("row")
    c = lax.axis_index("col")
    z = lax.rem(r, 2)
    partner = r + 1 - 2 * z
    root = r // 4
    quarter = lax.rem(r, 4)
    y = r // 8
    diagonal = y == c // 2
    off_diagonal = jnp.logical_not(diagonal)
    in_plane = lax.rem(r, 8)

    bar = pltpu.get_barrier_semaphore()
    pl.semaphore_signal(bar, inc=1, device_id=(partner, c), device_id_type=MESH)

    def greet_plane(k, _):
        m = lax.rem(r // 2 + k, 16)
        pl.semaphore_signal(bar, inc=1, device_id=(2 * m + z, c), device_id_type=MESH)
        return 0

    lax.fori_loop(1, 16, greet_plane, 0)

    def greet_left(k, _):
        @pl.when(jnp.logical_or(k != r, root != c))
        def _():
            pl.semaphore_signal(bar, inc=1, device_id=(k, root), device_id_type=MESH)

        return 0

    lax.fori_loop(0, 32, greet_left, 0)
    for a in range(4):
        @pl.when(jnp.logical_or(4 * c + a != r, root != c))
        def _():
            pl.semaphore_signal(bar, inc=1, device_id=(4 * c + a, root), device_id_type=MESH)

    @pl.when(off_diagonal)
    def _():
        for s in range(4):
            pl.semaphore_signal(
                bar, inc=1, device_id=(8 * y + lax.rem(4 * c + s, 8), root), device_id_type=MESH
            )

    @pl.when(diagonal)
    def _():
        for k in range(1, 4):
            pl.semaphore_signal(
                bar, inc=1, device_id=(8 * lax.rem(y + k, 4) + in_plane, c), device_id_type=MESH
            )

    pw_right = pw_t[32:64, :]
    pw_left = pw_t[0:32, :].astype(F32)

    normed = []
    for s in range(2):
        normed.append(normalize(al[s].astype(F32))[0])
    tails = []
    for s in range(2):
        ft = lax.dot_general(
            pw_right, normed[s].astype(BF16), (((1,), (1,)), ((), ())), preferred_element_type=F32
        )
        g_right[r, pl.ds(32 * s, 32), :] = ft[:, :128].astype(BF16)
        tails.append(ft[:, 128:192])
    g_right[r, pl.ds(64, 32), :] = jnp.concatenate(tails, axis=1).astype(BF16)
    lf = None
    for h in range(2):
        for s in range(2):
            rows = jnp.concatenate(
                [normed[s][q * ROWS + h * HALF : q * ROWS + h * HALF + HALF] for q in range(4)], axis=0
            ).astype(BF16)
            before = 32 * (2 * h + s)
            place = [jnp.zeros((n, 256), F32) for n in (before, 96 - before) if n]
            place.insert(1 if before else 0, pw_left)
            place = jnp.concatenate(place, axis=0).astype(BF16)
            term = lax.dot_general(rows, place, (((1,), (1,)), ((), ())), preferred_element_type=F32)
            lf = term if lf is None else lf + term
    for q in range(4):
        own_left[q] = jnp.concatenate(
            [lf[q * HALF : (q + 1) * HALF], jnp.zeros((8, 128), F32)], axis=0
        ).astype(BF16)

    is_root = (root == c).astype(jnp.int32)
    on_diagonal = diagonal.astype(jnp.int32)
    pl.semaphore_wait(bar, 53 - 2 * is_root + 11 * on_diagonal)

    def right_copy(block, slot, dest):
        return pltpu.make_async_remote_copy(
            src_ref=g_right.at[block], dst_ref=g_right.at[block],
            send_sem=right_send.at[slot], recv_sem=right_recv.at[block],
            device_id=(dest, c), device_id_type=MESH,
        )

    right_copy(r, 0, partner).start()

    def start_own(k, _):
        m = lax.rem(r // 2 + k, 16)
        right_copy(r, k, 2 * m + z).start()
        return 0

    lax.fori_loop(1, 16, start_own, 0)

    def left_copy(k):
        return pltpu.make_async_remote_copy(
            src_ref=own_left.at[k // 8], dst_ref=g_left.at[r],
            send_sem=left_send.at[k], recv_sem=left_recv.at[r],
            device_id=(4 * c + k // 8, lax.rem(k, 8)), device_id_type=MESH,
        )

    def left_self(k):
        return jnp.logical_and(4 * c + k // 8 == r, lax.rem(k, 8) == c)

    def start_left(k, _):
        mine = left_self(k)

        @pl.when(mine)
        def _():
            pltpu.make_async_copy(own_left.at[k // 8], g_left.at[r], left_recv.at[r]).start()

        @pl.when(jnp.logical_not(mine))
        def _():
            left_copy(k).start()

        return 0

    lax.fori_loop(0, 32, start_left, 0)

    for k in range(4):
        cols = slice(k * 128, (k + 1) * 128)
        half_shrink_t[:, cols] = (0.5 * w_shrink[cols, :].astype(F32)).T.astype(BF16)
        wide = w_expand[:, cols].astype(F32)
        expand_t[cols, :] = (wide - jnp.mean(wide, axis=0, keepdims=True)).T.astype(BF16)
    half_expand[...] = (0.5 * w_expand[...].astype(F32)).astype(BF16)
    wb = jnp.concatenate([w_bins_t[...].astype(F32), jnp.zeros((64, 128), F32)], axis=0)
    wb_high = jnp.concatenate([jnp.zeros((64, 128), F32), w_bins_t[...].astype(F32)], axis=0)
    bins2[0:128, :] = wb.T.astype(BF16)
    bins2[128:256, :] = wb_high.T.astype(BF16)
    bins2_t[:, 0:128] = wb.astype(BF16)
    bins2_t[:, 128:256] = wb_high.astype(BF16)
    mirror[0:1024, :] = w_outer[...].astype(F32)
    for k in range(8):
        block = jnp.concatenate([mirror[pl.ds(4 * k + e, 32, stride=32), :] for e in range(4)], axis=0)
        w_outer_t[:, k * 128 : (k + 1) * 128] = block.T.astype(BF16)
    aims = targets[...].astype(F32)
    aims = [aims[:, :128], jnp.concatenate([aims[:, 128:], jnp.zeros((ROWS, 64), F32)], axis=1)]
    mask_a = mask_rows[pl.ds(3 * c // 2, 1), :].astype(F32)
    mask_b = mask_rows[pl.ds(3 * c // 2 + 1, 1), :].astype(F32)
    swap_a, swap_b = pltpu.roll(mask_a, 64, axis=1), pltpu.roll(mask_b, 64, axis=1)
    odd = jnp.broadcast_to(lax.rem(c, 2), (1, 128)) == 1
    low_lane = lax.broadcasted_iota(jnp.int32, (1, 128), 1) < 64
    masks = [
        jnp.where(odd, jnp.where(low_lane, swap_a, swap_b), mask_a),
        jnp.where(odd, swap_b, mask_b),
    ]
    table = [
        jnp.concatenate([x, 2.0 * m, jnp.zeros((79, 128), F32)], axis=0).T for x, m in zip(aims, masks)
    ]
    goals[...] = permute(
        jnp.concatenate([table[0], table[1][:64]], axis=0), ORDER
    ).astype(BF16).reshape(3, CHUNK, 128)

    right_copy(partner, 0, partner).wait_recv()

    def start_partner(k, _):
        m = lax.rem(r // 2 + k, 16)
        right_copy(partner, 15 + k, 2 * m + z).start()
        return 0

    lax.fori_loop(1, 16, start_partner, 0)

    def wait_left(k, _):
        pltpu.make_async_copy(g_left.at[k], g_left.at[k], left_recv.at[k]).wait()
        return 0

    lax.fori_loop(0, 32, wait_left, 0)

    def left_rows(k, _):
        f_left[pl.ds(pl.multiple_of(k * 32, 32), 32), :] = g_left[k].astype(F32) * (1.0 / 64.0)
        return 0

    lax.fori_loop(0, 32, left_rows, 0)

    def left_block(p, _):
        x = f_left[pl.ds(p, 32, stride=32), :]
        stack = jnp.concatenate([x] + [pltpu.roll(x, 128 - 32 * g, axis=1) for g in range(1, 4)], axis=0)
        left_op[pl.ds(pl.multiple_of(p * 32, 32), 32), :] = stack.T[:32].astype(BF16)
        return 0

    lax.fori_loop(0, HALF, left_block, 0)

    def wait_right(k, _):
        m = lax.rem(r // 2 + k, 16)
        right_copy(2 * m + z, 0, partner).wait_recv()
        right_copy(2 * m + 1 - z, 0, partner).wait_recv()
        return 0

    lax.fori_loop(1, 16, wait_right, 0)

    def right_rows(k, _):
        f_right[pl.ds(pl.multiple_of(k * 96, 96), 96), :] = g_right[k].astype(F32)
        return 0

    lax.fori_loop(0, 32, right_rows, 0)

    low = lax.broadcasted_iota(jnp.int32, (32, 128), 1) < 64

    def right_step(e2, _):
        ab, tail = [], []
        zero = jnp.zeros((32, 128), F32)
        for par in range(2):
            e = 2 * e2 + par
            x0 = f_right[pl.ds(e, 32, stride=96), :]
            x1 = f_right[pl.ds(e + 32, 32, stride=96), :]
            xb = f_right[pl.ds(e + 64, 32, stride=96), :]
            xr = pltpu.roll(xb, 64, axis=1)
            h0 = jnp.concatenate([x0, x1, zero, zero], axis=0)
            h1 = jnp.concatenate([zero, zero, x0, x1], axis=0)
            ab.append(jnp.concatenate([h0, h1], axis=1).astype(BF16))
            tail.append(
                jnp.concatenate(
                    [
                        jnp.where(low, xb, zero), jnp.where(low, xr, zero),
                        jnp.where(low, zero, xr), jnp.where(low, zero, xb),
                    ],
                    axis=0,
                ).astype(BF16)
            )
        for n, chunk in enumerate(ab + [jnp.concatenate(tail, axis=1)]):
            right_op[e2, n] = chunk
        return 0

    lax.fori_loop(0, 16, right_step, 0)

    def outer_block(mb):
        def outer_step(e2, _):
            lhs = left_op[pl.ds(pl.multiple_of(mb * 256, 256), 256), :]
            for which in range(3):
                res = dot(lhs, right_op[e2, which]).astype(BF16)
                for pi in range(8):
                    pp = 4 * mb + pi // 2
                    piece = res[pi * 32 : (pi + 1) * 32]
                    if which < 2:
                        rows = pl.ds(pl.multiple_of((2 * e2 + which) * 32, 32), 32)
                        outer_op[pp, rows, pl.ds((pi % 2) * 384, 256)] = piece
                    else:
                        for par in range(2):
                            rows = pl.ds(pl.multiple_of((2 * e2 + par) * 32, 32), 32)
                            outer_op[pp, rows, pl.ds((pi % 2) * 384 + 256, 128)] = piece[
                                :, par * 128 : (par + 1) * 128
                            ]
            return 0

        lax.fori_loop(0, 16, outer_step, 0, unroll=OUTER_UNROLL)

    def mirror_copy(st, a):
        return pltpu.make_async_remote_copy(
            src_ref=logits.at[st, a],
            dst_ref=arrived.at[quarter, pl.ds(2 * st, 2)],
            send_sem=mir_send.at[st, a], recv_sem=mir_recv.at[st, quarter],
            device_id=(4 * c + a, root), device_id_type=MESH,
        )

    def mirror_is_self(a):
        return jnp.logical_and(4 * c + a == r, root == c)

    def relay_copy(st):
        return pltpu.make_async_remote_copy(
            src_ref=logits.at[st], dst_ref=relay.at[y, st],
            send_sem=relay_send.at[st], recv_sem=relay_recv.at[y, st],
            device_id=(8 * (c // 2) + in_plane, c), device_id_type=MESH,
        )

    def pass_copy(source, st, a):
        return pltpu.make_async_remote_copy(
            src_ref=relay.at[source, st, a],
            dst_ref=arrived.at[quarter, pl.ds(2 * st, 2)],
            send_sem=pass_send.at[source, st, a], recv_sem=mir_recv.at[st, quarter],
            device_id=(4 * c + a, 2 * source + in_plane // 4), device_id_type=MESH,
        )

    def goes_round(st):
        return lax.rem(st, 2) == 0

    def is_relayed(st):
        return jnp.logical_and(off_diagonal, goes_round(st))

    def pass_on(st):
        @pl.when(jnp.logical_and(diagonal, goes_round(st)))
        def _():
            for k in range(1, 4):
                source = lax.rem(y + k, 4)
                block = relay.at[source, st]
                pltpu.make_async_copy(block, block, relay_recv.at[source, st]).wait()
                for turn in range(4):
                    pass_copy(source, st, lax.rem(turn + quarter, 4)).start()

    def update_into(ref, st):
        upd_t = dot(w_outer_t[...], outer_op[st])
        for k in range(6):
            ref[k] = upd_t[:, k * 128 : (k + 1) * 128].T

    def forward_step(st, upd, later):
        update_into(later, st + 1 if later is upd_odd else jnp.minimum(st + 1, 11))
        order = [(t, h) for t in range(2) for h in range(2)]
        finals = []
        for g in range(0, 4, FORWARD_GROUP):
            group = order[g : g + FORWARD_GROUP]
            ids = [2 * st + t + HALF * h for t, h in group]
            sums = []
            for (t, h), i in zip(group, ids):
                update = jnp.concatenate([upd[3 * t + h], upd[3 * t + 2][h * 64 : (h + 1) * 64]], axis=0)
                sums.append(permute(pair[i].astype(F32) + update, ORDER))
            mid = jnp.concatenate(sums, axis=0).astype(BF16)
            for n, i in enumerate(ids):
                middle[i] = mid[n * COLS : (n + 1) * COLS].reshape(3, CHUNK, 128)
            mid = mid.astype(F32)
            xn = normalize(mid)[0].astype(BF16)
            half = dot(xn, half_expand[...]).astype(BF16).astype(F32)
            th = jnp.tanh(half)
            hid = half + half * th
            slopes = ((1.0 + th) + (hid - hid * th)).astype(BF16)
            for n, i in enumerate(ids):
                slope[i] = slopes[n * COLS : (n + 1) * COLS].reshape(3, CHUNK, HID)
            final = (mid + dot(hid.astype(BF16), w_shrink[...])).astype(BF16)
            finals += [final[n * COLS : (n + 1) * COLS] for n in range(FORWARD_GROUP)]
        wide = jnp.concatenate(
            [jnp.concatenate(finals[0:2], axis=1), jnp.concatenate(finals[2:4], axis=1)], axis=0
        )
        logit = dot(wide, bins2[...]).astype(BF16)
        for t in range(2):
            for k in range(3):
                for a in range(4):
                    at = t * COLS + k * CHUNK + a * 16
                    logits[st, a, t, k] = logit[at : at + 16]

    def send_step(st):
        @pl.when(is_relayed(st))
        def _():
            relay_copy(st).start()

        @pl.when(jnp.logical_not(is_relayed(st)))
        def _():
            for turn in range(4):
                a = lax.rem(turn + quarter + y, 4)
                mine = mirror_is_self(a)

                @pl.when(mine)
                def _():
                    pltpu.make_async_copy(
                        logits.at[st, a],
                        arrived.at[quarter, pl.ds(2 * st, 2)],
                        mir_recv.at[st, quarter],
                    ).start()

                @pl.when(jnp.logical_not(mine))
                def _():
                    mirror_copy(st, a).start()

        @pl.when(st >= LAG)
        def _():
            pass_on(st - LAG)

    outer_block(0)
    update_into(upd_even, 0)

    def forward_pair(k, _):
        @pl.when(jnp.logical_or(k == 1, k == 3))
        def _():
            outer_block((k + 1) // 2)

        forward_step(2 * k, upd_even, upd_odd)
        send_step(2 * k)
        forward_step(2 * k + 1, upd_odd, upd_even)
        send_step(2 * k + 1)
        return 0

    lax.fori_loop(0, 6, forward_pair, 0)
    for st in range(12 - LAG, 12):
        pass_on(jnp.int32(st))

    def take_mirror(st, _):
        for s in range(4):
            rows = arrived.at[s, pl.ds(2 * st, 2)]
            pltpu.make_async_copy(rows, rows, mir_recv.at[st, s]).wait()
            for t in range(2):
                q = 2 * st + t
                block = arrived[s, q].reshape(ROWS, 128).astype(F32)
                mirror[pl.ds(pl.multiple_of(s * 1152 + q * ROWS, 16), ROWS), :] = block
        return 0

    span = BACK_ROWS * CHUNK
    first = lax.broadcasted_iota(jnp.int32, (span, 128), 1) < 64
    code = lax.rem(lax.broadcasted_iota(jnp.int32, (span, 128), 1), 64).astype(F32)
    first_chunk = lax.broadcasted_iota(jnp.int32, (CHUNK, 128), 1) < 64
    small = lax.broadcasted_iota(jnp.int32, (8, 128), 1) < 64
    sel_row = lax.broadcasted_iota(jnp.int32, (128, 256), 0)
    sel_lane = lax.broadcasted_iota(jnp.int32, (128, 256), 1)
    sel_add = HALF * lax.rem(sel_lane // 64, 2) + sel_lane // 128

    def backward_rows(k, g):
        col_weight = jnp.broadcast_to(goals[k][:, 48:49].astype(F32), (CHUNK, 128))
        parts, weights, aims, own = [], [], [], []
        for n in range(BACK_ROWS):
            p = BACK_ROWS * g + n
            for s in range(4):
                at = s * 1152 + k * (8 * ROWS) + (p // 8) * 16 + lax.rem(p, 8)
                x0 = mirror[pl.ds(at, 8, stride=ROWS), :]
                x1 = mirror[pl.ds(at + 8, 8, stride=ROWS), :]
                parts.append(jnp.where(small, x0, pltpu.roll(x1, 64, axis=1)))
                parts.append(jnp.where(small, pltpu.roll(x0, 64, axis=1), x1))
            m0 = mask[r * ROWS + p].astype(F32)
            m1 = mask[r * ROWS + p + HALF].astype(F32)
            weights.append(col_weight * jnp.where(first_chunk, m0, m1))
            own += [logits[p // 2, a, n % 2, k].astype(F32) for a in range(4)]
            if n % 2 == 0:
                both = dot(goals[k], (sel_row == sel_add + p).astype(BF16))
                aims += [both[:, :128], both[:, 128:]]
        scores = jnp.concatenate(own, axis=0) + jnp.concatenate(parts, axis=0)
        low_max = jnp.max(jnp.where(first, scores, -jnp.inf), axis=-1, keepdims=True)
        high_max = jnp.max(jnp.where(first, -jnp.inf, scores), axis=-1, keepdims=True)
        expo = jnp.exp(scores - jnp.where(first, low_max, high_max))
        low_sum = jnp.sum(jnp.where(first, expo, 0.0), axis=-1, keepdims=True)
        high_sum = jnp.sum(jnp.where(first, 0.0, expo), axis=-1, keepdims=True)
        prob = expo * jnp.where(first, 1.0 / low_sum, 1.0 / high_sum)
        aim = jnp.concatenate(aims, axis=0)
        dlog = ((prob - jnp.where(aim == code, 1.0, 0.0)) * jnp.concatenate(weights, axis=0)).astype(BF16)
        dfin = dot(dlog, bins2_t[...])
        ids = [BACK_ROWS * g + n + HALF * h for h in range(2) for n in range(BACK_ROWS)]
        grad = jnp.concatenate([dfin[:, :128], dfin[:, 128:]], axis=0)
        slopes = jnp.concatenate([slope[i, k] for i in ids], axis=0)
        dh = (dot(grad.astype(BF16), half_shrink_t[...]) * slopes.astype(F32)).astype(BF16)
        dxn = dot(dh, expand_t[...])
        mid = jnp.concatenate([middle[i, k] for i in ids], axis=0)
        xhat, scale = normalize(mid.astype(F32))
        overlap = jnp.mean(dxn * xhat, axis=-1, keepdims=True)
        res = (grad + scale * (dxn - xhat * overlap)).astype(BF16)
        for n, i in enumerate(ids):
            out[i, k] = res[n * CHUNK : (n + 1) * CHUNK]

    def backward_chunk(k, _):
        lax.fori_loop(4 * k, 4 * k + 4, take_mirror, 0)

        def backward_step(g, _):
            backward_rows(k, g)
            return 0

        lax.fori_loop(0, HALF // BACK_ROWS, backward_step, 0, unroll=BACK_UNROLL)
        return 0

    lax.fori_loop(0, 3, backward_chunk, 0)

    def drain_right(k, _):
        right_copy(r, k, partner).wait_send()
        return 0

    lax.fori_loop(0, 31, drain_right, 0)

    def drain_left(k, _):
        @pl.when(jnp.logical_not(left_self(k)))
        def _():
            left_copy(k).wait_send()

        return 0

    lax.fori_loop(0, 32, drain_left, 0)

    def drain_mirror(st, _):
        @pl.when(is_relayed(st))
        def _():
            relay_copy(st).wait_send()

        @pl.when(jnp.logical_not(is_relayed(st)))
        def _():
            for a in range(4):
                @pl.when(jnp.logical_not(mirror_is_self(a)))
                def _():
                    mirror_copy(st, a).wait_send()

        return 0

    lax.fori_loop(0, 12, drain_mirror, 0)

    def drain_pass(st, _):
        @pl.when(jnp.logical_and(diagonal, goes_round(st)))
        def _():
            for k in range(1, 4):
                for a in range(4):
                    pass_copy(lax.rem(y + k, 4), st, a).wait_send()

        return 0

    lax.fori_loop(0, 12, drain_pass, 0)


def unpermute(grads, out):
    for i in range(grads.shape[0]):
        out[i] = permute(grads[i].reshape(COLS, CH).astype(F32), BACK_ORDER).astype(BF16)


def per_device(
    alignment, pair_act, targets, crop_mask, projection_weight, w_outer, w_expand, w_shrink, w_bins
):
    vmem = pl.BlockSpec(memory_space=pltpu.VMEM)
    grads = pl.pallas_call(
        kernel,
        out_shape=jax.ShapeDtypeStruct((ROWS, 3, CHUNK, CH), BF16),
        in_specs=[vmem] * 4 + [pl.BlockSpec(memory_space=pltpu.SMEM)] + [vmem] * 5,
        out_specs=vmem,
        scratch_shapes=[
            pltpu.VMEM((32, 96, 128), BF16),
            pltpu.VMEM((32, 32, 128), BF16),
            pltpu.VMEM((4, 32, 128), BF16),
            pltpu.VMEM((3072, 128), F32),
            pltpu.VMEM((1024, 128), F32),
            pltpu.VMEM((768, 128), BF16),
            pltpu.VMEM((16, 3, 128, 256), BF16),
            pltpu.VMEM((12, 1024, 768), BF16),
            pltpu.VMEM((ROWS, 3, CHUNK, CH), BF16),
            pltpu.VMEM((ROWS, 3, CHUNK, HID), BF16),
            pltpu.VMEM((12, 4, 2, 3, 16, 128), BF16),
            pltpu.VMEM((4, HALF, 3, 16, 128), BF16),
            pltpu.VMEM((4 * HALF * ROWS, 128), F32),
            pltpu.VMEM((4, 12, 4, 2, 3, 16, 128), BF16),
            pltpu.VMEM((128, 1024), BF16),
            pltpu.VMEM((128, HID), BF16),
            pltpu.VMEM((256, 128), BF16),
            pltpu.VMEM((128, HID), BF16),
            pltpu.VMEM((HID, 128), BF16),
            pltpu.VMEM((128, 256), BF16),
            pltpu.VMEM((3, CHUNK, 128), BF16),
            pltpu.VMEM((6, 128, 128), F32),
            pltpu.VMEM((6, 128, 128), F32),
            pltpu.SemaphoreType.DMA((31,)),
            pltpu.SemaphoreType.DMA((32,)),
            pltpu.SemaphoreType.DMA((32,)),
            pltpu.SemaphoreType.DMA((32,)),
            pltpu.SemaphoreType.DMA((12, 4)),
            pltpu.SemaphoreType.DMA((12, 4)),
            pltpu.SemaphoreType.DMA((12,)),
            pltpu.SemaphoreType.DMA((4, 12)),
            pltpu.SemaphoreType.DMA((4, 12, 4)),
        ],
        compiler_params=pltpu.CompilerParams(
            collective_id=0, has_side_effects=True, vmem_limit_bytes=63 * 1024 * 1024
        ),
    )(
        alignment, pair_act, targets, crop_mask.reshape(12, 128), crop_mask, projection_weight.T,
        w_outer, w_expand, w_shrink, w_bins.T,
    )
    return pl.pallas_call(
        unpermute,
        grid=(ROWS // EMIT_ROWS,),
        out_shape=jax.ShapeDtypeStruct((ROWS, COLS, CH), BF16),
        in_specs=[pl.BlockSpec((EMIT_ROWS, 3, CHUNK, CH), lambda i: (i, 0, 0, 0))],
        out_specs=pl.BlockSpec((EMIT_ROWS, COLS, CH), lambda i: (i, 0, 0)),
    )(grads)


def solution(mesh):
    in_specs = (
        P("row", "col", None), P("row", "col", None), P("row", "col"),
        P(), P(), P(), P(), P(), P(),
    )
    return jax.shard_map(
        per_device, mesh=mesh, in_specs=in_specs, out_specs=P("row", "col", None), check_vma=False
    )
```

time: 108 us -> 94.3 us (0.87)
  local copies, waits for them, and re-layouts: 7.49 us -> 0 us
  Pallas kernels: 100 us -> 94.1 us
    pallas_call x1 -> x2, Pallas kernels: 100 us -> 94.1 us  [the longest x1 90.1 us: per_device(): pl.pallas_call(kernel, out_shape=jax.ShapeDtypeStruct((ROWS, 3, CHUNK, CH...]
    unnamed x3 -> x0, local copies, waits for them, and re-layouts: 6.13 us -> none
    reshape x1 -> x0, local copies, waits for them, and re-layouts: 1.36 us -> none  [per_device(): crop_mask.reshape(8, COLS)]
where the time goes in v3:
time: 94.3 us; the launch traced here: 94.1 us
  Pallas kernels  94.1 us (100%)
    pallas_call x1, Pallas kernels, per_device(): pl.pallas_call(kernel, out_shape=jax.ShapeDtypeStruct((ROWS, 3, CHUNK, CH...  90.1 us
    pallas_call x1, Pallas kernels, per_device(): pl.pallas_call(unpermute, grid=(ROWS // EMIT_ROWS,), out_shape=jax.ShapeD...  4.01 us

profile of v3, /device:TPU:1, one launch (start us, length us, event | category | flops | bytes accessed | tf_op | source)
XLA Modules:
  0.0 94.1 jit_solution(6326891854095288358)
XLA Ops:
  0.0 90.1 %shard_map.91.grads = bf16[48,3,64,128]{3,2,1,0:T(8,128)(2,1)} custom-call(bf16[2,192,256]{2,1,0:T(8,128)(2,1)} %al.1, bf16[48,192,128]{2,1,0:T(8,128)(2,1)} %pair.1, s32[48,192]{1,0:T(8,128)} %targets.1, s32[12,128]{1,0:T(8,128)} %bitcast.4, s32[1536]{0:T(1024)} %mask.1, bf16[64,256]{1,0:T(8,128)(2,1)} %bitcast.3, bf16[1024,128]{1,0:T(8,128)(2,1)} %w_outer.1, ...), custom_call_target="tpu_custom_call" | custom-call | tf_op jit(solution)/shard_map/pallas_call | solution.py:552
  90.1 4.0 %shard_map.92 = bf16[48,192,128]{2,1,0:T(8,128)(2,1)} custom-call(bf16[48,3,64,128]{3,2,1,0:T(8,128)(2,1)} %shard_map.91.grads), custom_call_target="tpu_custom_call" | custom-call | tf_op jit(solution)/shard_map/pallas_call | solution.py:598

commit v4 on v3

--- a/solution.py
+++ b/solution.py
@@ -16,13 +16,13 @@
 HID = 512
 OUTER_BLOCKS = 1
 FORWARD_GROUP = 4
-BACK_ROWS = 8
+BACK_ROWS = 4
 CHUNK = 64
-EMIT_ROWS = 12
+EMIT_ROWS = 24
 RELAYED = 6
-LAG = 2
+LAG = 1
 OUTER_UNROLL = 2
-BACK_UNROLL = 1
+BACK_UNROLL = 3
 ORDER = [a * 6 + h * 3 + k for k in range(3) for a in range(4) for h in range(2)]
 BACK_ORDER = [ORDER.index(n) for n in range(24)]
 
@@ -43,10 +43,10 @@
 
 
 def kernel(
-    al, pair, targets, mask_rows, mask, pw_t, w_outer, w_expand, w_shrink, w_bins_t,
-    out,
+    al, pair_hbm, targets, mask_rows, mask, pw_t, w_outer, w_expand, w_shrink, w_bins_t,
+    out_hbm,
     g_right, g_left, own_left, f_right, f_left, left_op, right_op, outer_op, middle, slope, logits, arrived, mirror,
-    relay, w_outer_t, half_expand, bins2, half_shrink_t, expand_t, bins2_t, goals, upd_even, upd_odd,
+    relay, w_outer_t, half_expand, bins2, half_shrink_t, expand_t, bins2_t, goals, upd_even, upd_odd, pair, grads, pair_sem, out_sem,
     right_send, right_recv, left_send, left_recv, mir_send, mir_recv, relay_send, relay_recv, pass_send,
 ):
     r = lax.axis_index("row")
@@ -59,6 +59,9 @@
     diagonal = y == c // 2
     off_diagonal = jnp.logical_not(diagonal)
     in_plane = lax.rem(r, 8)
+
+    pair_copy = pltpu.make_async_copy(pair_hbm, pair, pair_sem)
+    pair_copy.start()
 
     bar = pltpu.get_barrier_semaphore()
     pl.semaphore_signal(bar, inc=1, device_id=(partner, c), device_id_type=MESH)
@@ -236,23 +239,31 @@
 
     lax.fori_loop(0, HALF, left_block, 0)
 
+    def take_right(block):
+        f_right[pl.ds(pl.multiple_of(block * 96, 96), 96), :] = g_right[block].astype(F32)
+
+    take_right(r)
+    take_right(partner)
+
     def wait_right(k, _):
         m = lax.rem(r // 2 + k, 16)
         right_copy(2 * m + z, 0, partner).wait_recv()
+        take_right(2 * m + z)
+        return 0
+
+    lax.fori_loop(1, 16, wait_right, 0)
+
+    def wait_other(k, _):
+        m = lax.rem(r // 2 + k, 16)
         right_copy(2 * m + 1 - z, 0, partner).wait_recv()
-        return 0
-
-    lax.fori_loop(1, 16, wait_right, 0)
-
-    def right_rows(k, _):
-        f_right[pl.ds(pl.multiple_of(k * 96, 96), 96), :] = g_right[k].astype(F32)
-        return 0
-
-    lax.fori_loop(0, 32, right_rows, 0)
+        take_right(2 * m + 1 - z)
+        return 0
+
+    lax.fori_loop(1, 16, wait_other, 0)
 
     low = lax.broadcasted_iota(jnp.int32, (32, 128), 1) < 64
 
-    def right_step(e2, _):
+    def right_chunks(e2):
         ab, tail = [], []
         zero = jnp.zeros((32, 128), F32)
         for par in range(2):
@@ -273,29 +284,35 @@
                     axis=0,
                 ).astype(BF16)
             )
-        for n, chunk in enumerate(ab + [jnp.concatenate(tail, axis=1)]):
-            right_op[e2, n] = chunk
-        return 0
-
-    lax.fori_loop(0, 16, right_step, 0)
+        return ab + [jnp.concatenate(tail, axis=1)]
+
+    def outer_rows(mb, e2, chunks):
+        lhs = left_op[pl.ds(pl.multiple_of(mb * 128, 128), 128), :]
+        for which in range(3):
+            res = dot(lhs, chunks[which]).astype(BF16)
+            for pi in range(4):
+                pp = 2 * mb + pi // 2
+                piece = res[pi * 32 : (pi + 1) * 32]
+                if which < 2:
+                    rows = pl.ds(pl.multiple_of((2 * e2 + which) * 32, 32), 32)
+                    outer_op[pp, rows, pl.ds((pi % 2) * 384, 256)] = piece
+                else:
+                    for par in range(2):
+                        rows = pl.ds(pl.multiple_of((2 * e2 + par) * 32, 32), 32)
+                        outer_op[pp, rows, pl.ds((pi % 2) * 384 + 256, 128)] = piece[
+                            :, par * 128 : (par + 1) * 128
+                        ]
+
+    def first_outer(e2, _):
+        chunks = right_chunks(e2)
+        for n in range(3):
+            right_op[e2, n] = chunks[n]
+        outer_rows(0, e2, chunks)
+        return 0
 
     def outer_block(mb):
         def outer_step(e2, _):
-            lhs = left_op[pl.ds(pl.multiple_of(mb * 256, 256), 256), :]
-            for which in range(3):
-                res = dot(lhs, right_op[e2, which]).astype(BF16)
-                for pi in range(8):
-                    pp = 4 * mb + pi // 2
-                    piece = res[pi * 32 : (pi + 1) * 32]
-                    if which < 2:
-                        rows = pl.ds(pl.multiple_of((2 * e2 + which) * 32, 32), 32)
-                        outer_op[pp, rows, pl.ds((pi % 2) * 384, 256)] = piece
-                    else:
-                        for par in range(2):
-                            rows = pl.ds(pl.multiple_of((2 * e2 + par) * 32, 32), 32)
-                            outer_op[pp, rows, pl.ds((pi % 2) * 384 + 256, 128)] = piece[
-                                :, par * 128 : (par + 1) * 128
-                            ]
+            outer_rows(mb, e2, [right_op[e2, n] for n in range(3)])
             return 0
 
         lax.fori_loop(0, 16, outer_step, 0, unroll=OUTER_UNROLL)
@@ -408,16 +425,18 @@
         def _():
             pass_on(st - LAG)
 
-    outer_block(0)
+    lax.fori_loop(0, 16, first_outer, 0, unroll=OUTER_UNROLL)
+    pair_copy.wait()
     update_into(upd_even, 0)
 
     def forward_pair(k, _):
-        @pl.when(jnp.logical_or(k == 1, k == 3))
-        def _():
-            outer_block((k + 1) // 2)
-
         forward_step(2 * k, upd_even, upd_odd)
         send_step(2 * k)
+
+        @pl.when(k < 5)
+        def _():
+            outer_block(k + 1)
+
         forward_step(2 * k + 1, upd_odd, upd_even)
         send_step(2 * k + 1)
         return 0
@@ -483,7 +502,7 @@
         overlap = jnp.mean(dxn * xhat, axis=-1, keepdims=True)
         res = (grad + scale * (dxn - xhat * overlap)).astype(BF16)
         for n, i in enumerate(ids):
-            out[i, k] = res[n * CHUNK : (n + 1) * CHUNK]
+            grads[k, i] = res[n * CHUNK : (n + 1) * CHUNK]
 
     def backward_chunk(k, _):
         lax.fori_loop(4 * k, 4 * k + 4, take_mirror, 0)
@@ -493,9 +512,13 @@
             return 0
 
         lax.fori_loop(0, HALF // BACK_ROWS, backward_step, 0, unroll=BACK_UNROLL)
+        pltpu.make_async_copy(grads.at[k], out_hbm.at[k], out_sem.at[k]).start()
         return 0
 
     lax.fori_loop(0, 3, backward_chunk, 0)
+
+    for k in range(3):
+        pltpu.make_async_copy(grads.at[k], out_hbm.at[k], out_sem.at[k]).wait()
 
     def drain_right(k, _):
         right_copy(r, k, partner).wait_send()
@@ -541,19 +564,21 @@
 
 
 def unpermute(grads, out):
-    for i in range(grads.shape[0]):
-        out[i] = permute(grads[i].reshape(COLS, CH).astype(F32), BACK_ORDER).astype(BF16)
+    for i in range(out.shape[0]):
+        rows = jnp.concatenate([grads[k, i].astype(F32) for k in range(3)], axis=0)
+        out[i] = permute(rows, BACK_ORDER).astype(BF16)
 
 
 def per_device(
     alignment, pair_act, targets, crop_mask, projection_weight, w_outer, w_expand, w_shrink, w_bins
 ):
     vmem = pl.BlockSpec(memory_space=pltpu.VMEM)
+    anywhere = pl.BlockSpec(memory_space=pl.ANY)
     grads = pl.pallas_call(
         kernel,
-        out_shape=jax.ShapeDtypeStruct((ROWS, 3, CHUNK, CH), BF16),
-        in_specs=[vmem] * 4 + [pl.BlockSpec(memory_space=pltpu.SMEM)] + [vmem] * 5,
-        out_specs=vmem,
+        out_shape=jax.ShapeDtypeStruct((3, ROWS, CHUNK, CH), BF16),
+        in_specs=[vmem, anywhere, vmem, vmem] + [pl.BlockSpec(memory_space=pltpu.SMEM)] + [vmem] * 5,
+        out_specs=anywhere,
         scratch_shapes=[
             pltpu.VMEM((32, 96, 128), BF16),
             pltpu.VMEM((32, 32, 128), BF16),
@@ -578,6 +603,10 @@
             pltpu.VMEM((3, CHUNK, 128), BF16),
             pltpu.VMEM((6, 128, 128), F32),
             pltpu.VMEM((6, 128, 128), F32),
+            pltpu.VMEM((ROWS, COLS, CH), BF16),
+            pltpu.VMEM((3, ROWS, CHUNK, CH), BF16),
+            pltpu.SemaphoreType.DMA(()),
+            pltpu.SemaphoreType.DMA((3,)),
             pltpu.SemaphoreType.DMA((31,)),
             pltpu.SemaphoreType.DMA((32,)),
             pltpu.SemaphoreType.DMA((32,)),
@@ -599,7 +628,7 @@
         unpermute,
         grid=(ROWS // EMIT_ROWS,),
         out_shape=jax.ShapeDtypeStruct((ROWS, COLS, CH), BF16),
-        in_specs=[pl.BlockSpec((EMIT_ROWS, 3, CHUNK, CH), lambda i: (i, 0, 0, 0))],
+        in_specs=[pl.BlockSpec((3, EMIT_ROWS, CHUNK, CH), lambda i: (0, i, 0, 0))],
         out_specs=pl.BlockSpec((EMIT_ROWS, COLS, CH), lambda i: (i, 0, 0)),
     )(grads)
 

time: 94.3 us -> 85.6 us (0.908)
  Pallas kernels: 94.1 us -> 85.4 us
    pallas_call x1, Pallas kernels: 90.1 us -> 82.5 us  [per_device(): pl.pallas_call(kernel, out_shape=jax.ShapeDtypeStruct((3, ROWS, CHUNK, CH...]
    pallas_call x1, Pallas kernels: 4.01 us -> 2.89 us  [per_device(): pl.pallas_call(unpermute, grid=(ROWS // EMIT_ROWS,), out_shape=jax.ShapeD...]
where the time goes in v4:
time: 85.6 us; the launch traced here: 85.4 us
  Pallas kernels  85.4 us (100%)
    pallas_call x1, Pallas kernels, per_device(): pl.pallas_call(kernel, out_shape=jax.ShapeDtypeStruct((3, ROWS, CHUNK, CH...  82.5 us
    pallas_call x1, Pallas kernels, per_device(): pl.pallas_call(unpermute, grid=(ROWS // EMIT_ROWS,), out_shape=jax.ShapeD...  2.89 us

profile of v4, /device:TPU:1, one launch (start us, length us, event | category | flops | bytes accessed | tf_op | source)
XLA Modules:
  0.0 85.4 jit_solution(14444805338994806329)
XLA Ops:
  0.0 82.5 %shard_map.91.grads = bf16[3,48,64,128]{3,2,1,0:T(8,128)(2,1)} custom-call(bf16[2,192,256]{2,1,0:T(8,128)(2,1)} %al.1, bf16[48,192,128]{2,1,0:T(8,128)(2,1)} %pair_hbm.1, s32[48,192]{1,0:T(8,128)} %targets.1, s32[12,128]{1,0:T(8,128)} %bitcast.4, s32[1536]{0:T(1024)} %mask.1, bf16[64,256]{1,0:T(8,128)(2,1)} %bitcast.3, bf16[1024,128]{1,0:T(8,128)(2,1)} %w_outer.1, ...), custom_call_target="tpu_custom_call" | custom-call | tf_op jit(solution)/shard_map/pallas_call | solution.py:577
  82.6 2.9 %shard_map.92 = bf16[48,192,128]{2,1,0:T(8,128)(2,1)} custom-call(bf16[3,48,64,128]{3,2,1,0:T(8,128)(2,1)} %shard_map.91.grads), custom_call_target="tpu_custom_call" | custom-call | tf_op jit(solution)/shard_map/pallas_call | solution.py:627

commit v5 on v4

--- a/solution.py
+++ b/solution.py
@@ -315,7 +315,7 @@
             outer_rows(mb, e2, [right_op[e2, n] for n in range(3)])
             return 0
 
-        lax.fori_loop(0, 16, outer_step, 0, unroll=OUTER_UNROLL)
+        lax.fori_loop(0, 16, outer_step, 0, unroll=4)
 
     def mirror_copy(st, a):
         return pltpu.make_async_remote_copy(
@@ -425,7 +425,7 @@
         def _():
             pass_on(st - LAG)
 
-    lax.fori_loop(0, 16, first_outer, 0, unroll=OUTER_UNROLL)
+    lax.fori_loop(0, 16, first_outer, 0, unroll=4)
     pair_copy.wait()
     update_into(upd_even, 0)
 
@@ -583,8 +583,8 @@
             pltpu.VMEM((32, 96, 128), BF16),
             pltpu.VMEM((32, 32, 128), BF16),
             pltpu.VMEM((4, 32, 128), BF16),
-            pltpu.VMEM((3072, 128), F32),
-            pltpu.VMEM((1024, 128), F32),
+            pltpu.VMEM((3072 + 96, 128), F32),
+            pltpu.VMEM((1024 + 32, 128), F32),
             pltpu.VMEM((768, 128), BF16),
             pltpu.VMEM((16, 3, 128, 256), BF16),
             pltpu.VMEM((12, 1024, 768), BF16),
@@ -592,7 +592,7 @@
             pltpu.VMEM((ROWS, 3, CHUNK, HID), BF16),
             pltpu.VMEM((12, 4, 2, 3, 16, 128), BF16),
             pltpu.VMEM((4, HALF, 3, 16, 128), BF16),
-            pltpu.VMEM((4 * HALF * ROWS, 128), F32),
+            pltpu.VMEM((4 * HALF * ROWS + ROWS, 128), F32),
             pltpu.VMEM((4, 12, 4, 2, 3, 16, 128), BF16),
             pltpu.VMEM((128, 1024), BF16),
             pltpu.VMEM((128, HID), BF16),

time: 85.6 us -> 85.1 us (level)
  no operation moved by 1% of the time
where the time goes in v5:
time: 85.1 us; the launch traced here: 85 us
  Pallas kernels  85 us (100%)
    pallas_call x1, Pallas kernels, per_device(): pl.pallas_call(kernel, out_shape=jax.ShapeDtypeStruct((3, ROWS, CHUNK, CH...  82.1 us
    pallas_call x1, Pallas kernels, per_device(): pl.pallas_call(unpermute, grid=(ROWS // EMIT_ROWS,), out_shape=jax.ShapeD...  2.89 us

profile of v5, /device:TPU:1, one launch (start us, length us, event | category | flops | bytes accessed | tf_op | source)
XLA Modules:
  0.0 85.0 jit_solution(762220937766908777)
XLA Ops:
  0.0 82.1 %shard_map.91.grads = bf16[3,48,64,128]{3,2,1,0:T(8,128)(2,1)} custom-call(bf16[2,192,256]{2,1,0:T(8,128)(2,1)} %al.1, bf16[48,192,128]{2,1,0:T(8,128)(2,1)} %pair_hbm.1, s32[48,192]{1,0:T(8,128)} %targets.1, s32[12,128]{1,0:T(8,128)} %bitcast.4, s32[1536]{0:T(1024)} %mask.1, bf16[64,256]{1,0:T(8,128)(2,1)} %bitcast.3, bf16[1024,128]{1,0:T(8,128)(2,1)} %w_outer.1, ...), custom_call_target="tpu_custom_call" | custom-call | tf_op jit(solution)/shard_map/pallas_call | solution.py:577
  82.1 2.9 %shard_map.92 = bf16[48,192,128]{2,1,0:T(8,128)(2,1)} custom-call(bf16[3,48,64,128]{3,2,1,0:T(8,128)(2,1)} %shard_map.91.grads), custom_call_target="tpu_custom_call" | custom-call | tf_op jit(solution)/shard_map/pallas_call | solution.py:627
